TPU v7x, 32 devices: a whole 2x2x4 slice. The times are simulated.
32 devices in a mesh: groups: 2 (over x), col: 16 (over z, y, core).
Axes of the slice: x: 2, y: 2, z: 4, core: 2. Of those that a mesh axis runs over, the one named last changes fastest.
Arguments:
- left_features: bfloat16 [32, 8, 8192], P(None, None, ('groups', 'col')), parts along dimension 2, may hold values from -3 to 3
- right_features: bfloat16 [32, 8, 8192], P(None, None, ('groups', 'col')), parts along dimension 2, may hold values from -3 to 3
- tile_offsets: int32 [32], P(('groups', 'col')), parts along dimension 0, may hold values from 0 to 3
- valid_mask: int32 [8, 8192], P(None, ('groups', 'col')), parts along dimension 1, may hold values 0 or 1
Outputs:
- disparity: float32 [8, 8192], P(None, ('groups', 'col')), parts along dimension 1
- final_volume: bfloat16 [192, 8, 8192], P(None, None, ('groups', 'col')), parts along dimension 2
There are 2 independent parts, one for each index of `groups`. A program takes and returns all parts, laid end to end along the dimension named above; each array names one. Nothing has to cross between parts.
All inputs are finite; a program needn't handle non-finite values. No bound on the sum of `valid_mask` on one device may be relied on, other than what follows from the above.
Results may differ from a plain program's by a relative error of at most 0.001.
Values may be sent and summed in bfloat16 or wider, within the bound.
A program may use at most 64 MiB of HBM per device.

v0:
```python
import functools
import math

import jax
import jax.numpy as jnp
from jax import lax
from jax.experimental import pallas as pl
from jax.experimental.pallas import tpu as pltpu
from jax.sharding import PartitionSpec as P

D = 192
ITERS = 4
FLOOR_COST = -4.0
LANES = 128
SUB = 8
MESH = pl.DeviceIdType.MESH
STEPS = tuple((a, b) for a in (-1, 0, 1) for b in (-1, 0, 1))
PITCH = D + 8
GROUP = 32
PER = LANES // GROUP
BLOCKS = D // PER
LOG2E = math.log2(math.e)
FIRST_UNROLL = 48
UNROLL = 192
STRIP_UNROLL = 48
ROW_UNROLL = 8
CHANNEL_UNROLL = 32
VMEM_LIMIT = 24 * 1024 * 1024


def lroll(x, shift):
    shift = shift % x.shape[-1]
    return x if shift == 0 else pltpu.roll(x, shift, x.ndim - 1)


def sroll(x, shift):
    shift = shift % x.shape[-2]
    return x if shift == 0 else pltpu.roll(x, shift, x.ndim - 2)


def iota(shape, dim):
    return lax.broadcasted_iota(jnp.int32, shape, dim)


def distances(plane):
    right = lroll(plane, -1)
    others = (right, sroll(plane, -1), sroll(right, -1), sroll(lroll(plane, 1), -1))
    return tuple((plane - other) ** 2 for other in others) + (plane * plane,)


def affinity(sums, channels):
    across, down, down_right, down_left, norm = sums
    row = iota(across.shape, 0)
    first, last = row == 0, row == across.shape[0] - 1
    dist = {(1, 0): across, (-1, 0): lroll(across, 1)}
    for a, base in ((1, down_right), (0, down), (-1, down_left)):
        dist[a, 1] = jnp.where(last, norm, base)
        dist[-a, -1] = jnp.where(first, norm, sroll(lroll(base, a), 1))
    e = {k: jnp.exp(-d / (2.0 * channels)) for k, d in dist.items()}
    e[0, 0] = jnp.ones_like(across)
    total = sum(e[k] for k in STEPS)
    out = {k: e[k] / total for k in STEPS}
    for a in (-1, 0, 1):
        out[a, 1] = jnp.where(last, 0.0, out[a, 1])
        out[a, -1] = jnp.where(first, 0.0, out[a, -1])
    return out


def coefficients(weights, usable, s1, s2):
    purity = D * s2 / (s1 * s1)
    gating = purity / (1.0 + purity)
    part = 0.25 * usable * (1.0 - gating)
    return {k: lroll(weights[k] * part, k[0]) for k in STEPS}, usable * gating


def columns(w, above, mid, below):
    return [w[a, -1] * above + w[a, 0] * mid + w[a, 1] * below for a in (-1, 0, 1)]


def three(ref, s):
    at = (s + 1) * SUB
    return ref[at - 1 : at - 1 + SUB, :], ref[at : at + SUB, :], ref[at + 1 : at + 1 + SUB, :]


def pack(planes):
    lane = iota((SUB, LANES), 1)
    place = lane % GROUP
    out = jnp.zeros((SUB, LANES), jnp.float32)
    for s, (head, tail) in enumerate(planes):
        mine = lane // GROUP == s
        out = jnp.where(mine & (place >= 4) & (place < 16), lroll(head, GROUP * s + 4), out)
        out = jnp.where(mine & (place >= 16) & (place < 28), lroll(tail, GROUP * s + 16 - 116), out)
    return out


def step(v, st, w_ref, usable, vol_ref, sums):
    last = vol_ref is not None
    lane = iota((SUB, LANES), 1)
    head_lane, tail_lane = lane == 0, lane == LANES - 1
    none = jnp.zeros((SUB, LANES), jnp.float32)
    wide = lambda a, b: jnp.concatenate([a, b], axis=1)
    w, keep_own = coefficients(
        {k: w_ref[i] for i, k in enumerate(STEPS)}, usable,
        wide(sums[0], sums[2]), wide(sums[1], sums[3]),
    )
    cut = lambda x, t: x[:, t * LANES : (t + 1) * LANES]
    w = [{k: cut(w[k], t) for k in STEPS} for t in range(2)]
    keep_own = [cut(keep_own, t) for t in range(2)]

    def pooled(refs, s):
        z, mid = [], []
        for t in range(2):
            rows = three(refs[t], s)
            mid.append(rows[1])
            z.append(columns(w[t], *rows))
        r = [lroll(z[t][0], 1) for t in range(2)]
        l = [lroll(z[t][2], -1) for t in range(2)]
        r[1] = jnp.where(head_lane, r[0], r[1])
        l[0] = jnp.where(tail_lane, l[1], l[0])
        return [z[t][1] + (r[t] + l[t]) for t in range(2)], mid

    def finish(b, s, pair, sums):
        j = b * UNROLL + s
        pair, sums = list(pair), list(sums)
        if last:
            group = s % PER
            row = pl.multiple_of((b * (UNROLL // PER) + s // PER + 1) * SUB, SUB)
            strip = st[pl.ds(row, SUB), :]
            pair[0] = jnp.where(lane < 4, lroll(strip, -(GROUP * group + 4)), pair[0])
            pair[1] = jnp.where(lane >= LANES - 4, lroll(strip, 100 - GROUP * group), pair[1])
            out = jnp.concatenate(pair, axis=1) * (1.0 / LOG2E)
            vol_ref[D - 1 - j] = out.astype(jnp.bfloat16)
            level = (D - 1 - j).astype(jnp.float32) * (1.0 / D)
        for t in range(2):
            if not last:
                v[t, pl.ds(pl.multiple_of((j + 1) * SUB, SUB), SUB), :] = pair[t]
            e = jnp.exp2(pair[t])
            sums[2 * t] += e
            sums[2 * t + 1] += e * (level if last else e)
        return sums

    def advance(refs, b, s, carry):
        p_prev, s_prev, v_prev, acc = carry
        p, mid = pooled(refs, s)
        s_now = [p_prev[t] + p[t] for t in range(2)]
        new = [keep_own[t] * v_prev[t] + (s_prev[t] + s_now[t]) for t in range(2)]
        before = (b - 1, UNROLL - 1) if s == 0 else (b, s - 1)
        return p, s_now, mid, finish(*before, new, acc)

    def block_refs(b):
        at = pl.ds(pl.multiple_of(b * (UNROLL * SUB), SUB), (UNROLL + 2) * SUB)
        return [v.at[t, at, :] for t in range(2)]

    def loop(b, carry):
        p, s, m, acc = carry
        carry = list(p), list(s), list(m), list(acc)
        refs = block_refs(b)
        for k in range(UNROLL):
            carry = advance(refs, b, k, carry)
        return tuple(tuple(c) for c in carry)

    refs = block_refs(0)
    p, mid = pooled(refs, 0)
    carry = p, [2.0 * x for x in p], mid, [none] * 4
    for k in range(1, UNROLL):
        carry = advance(refs, jnp.int32(0), k, carry)
    carry = tuple(tuple(c) for c in carry)
    p_prev, s_prev, v_prev, acc = lax.fori_loop(1, D // UNROLL, loop, carry)
    new = [keep_own[t] * v_prev[t] + (s_prev[t] + 2.0 * p_prev[t]) for t in range(2)]
    return tuple(finish(jnp.int32(D // UNROLL - 1), UNROLL - 1, new, acc))


def kernel(
    n, left_ref, right_ref, offs_ref, mask_ref, v, st, w_ref, sums_ref,
    prev, lf, rs, t4, u, own, sent, from_left, from_right, send_sem, recv_sem,
):
    channels = left_ref.shape[0]
    tile = left_ref.shape[2]
    me = lax.axis_index("col")
    has_left, has_right = me > 0, me < n - 1
    lane = iota((SUB, LANES), 1)

    barrier = pltpu.get_barrier_semaphore()

    @pl.when(has_left)
    def _():
        pl.semaphore_signal(barrier, inc=1, device_id={"col": me - 1}, device_id_type=MESH)

    @pl.when(has_right)
    def _():
        pl.semaphore_signal(barrier, inc=1, device_id={"col": me + 1}, device_id_type=MESH)

    pl.semaphore_wait(barrier, has_left.astype(jnp.int32) + has_right.astype(jnp.int32))

    def remote(src, dst, slot, to):
        return pltpu.make_async_remote_copy(
            src_ref=src, dst_ref=dst, send_sem=send_sem.at[slot], recv_sem=recv_sem.at[slot],
            device_id={"col": to}, device_id_type=MESH,
        )

    tile_copy = remote(right_ref, prev, 0, me + 1)
    strip_right = remote(sent, from_left, 1, me + 1)
    strip_left = remote(sent, from_right, 2, me - 1)

    @pl.when(has_right)
    def _():
        tile_copy.start()

    @pl.when(jnp.logical_not(has_left))
    def _():
        prev[...] = jnp.zeros(prev.shape, prev.dtype)
        from_left[...] = jnp.zeros(from_left.shape, jnp.float32)

    @pl.when(jnp.logical_not(has_right))
    def _():
        from_right[...] = jnp.zeros(from_right.shape, jnp.float32)

    usable = mask_ref[...].astype(jnp.float32)

    zero = jnp.zeros((SUB, tile), jnp.float32)

    def channel(c, sums):
        plane = left_ref[c].astype(jnp.float32)
        at = pl.ds(pl.multiple_of(c * SUB, SUB), SUB)
        lf[0, at, :] = plane[:, :LANES]
        lf[1, at, :] = plane[:, LANES:]
        return tuple(s + d for s, d in zip(sums, distances(plane)))

    per = CHANNEL_UNROLL

    def unrolled(body):
        def run(i, carry):
            for k in range(per):
                carry = body(i * per + k, carry)
            return carry

        return run

    weights = affinity(lax.fori_loop(0, channels // per, unrolled(channel), (zero,) * 5), channels)
    for i, k in enumerate(STEPS):
        w_ref[i] = weights[k]

    for q in range(channels // PER):
        planes = [
            (lf[0, (q * PER + s) * SUB : (q * PER + s + 1) * SUB, :],
             lf[1, (q * PER + s) * SUB : (q * PER + s + 1) * SUB, :])
            for s in range(PER)
        ]
        own[BLOCKS + q] = pack(planes)
    mask_at = BLOCKS + channels // PER
    own[mask_at] = pack([(usable[:, :LANES], usable[:, LANES:])] * PER)
    for q in range(mask_at + 1, own.shape[0]):
        own[q] = jnp.zeros((SUB, LANES), jnp.float32)

    @pl.when(has_left)
    def _():
        tile_copy.wait_recv()

    def shifts(c, carry):
        at = pl.ds(pl.multiple_of(c * SUB, SUB), SUB)
        before = prev[c].astype(jnp.float32)
        mine = right_ref[c].astype(jnp.float32)
        parts = (before[:, :LANES], before[:, LANES:], mine[:, :LANES], mine[:, LANES:])
        for s in range(4):
            rolled = [lroll(p, -s) for p in parts]
            for t in range(4):
                value = rolled[t]
                if s and t < 3:
                    value = jnp.where(lane < LANES - s, value, rolled[t + 1])
                rs[s, t, at, :] = value
        return carry

    lax.fori_loop(0, channels // per, unrolled(shifts), 0)

    depth = 8 * channels
    keep = (iota((depth, tile), 0) // channels == iota((depth, tile), 1) % 8).astype(jnp.bfloat16)
    rows_out = tile - 8 + D
    begin = tile - D + 1

    def row(i, carry):
        for h in range(ROW_UNROLL):
            y = i * ROW_UNROLL + h
            for t in range(4):
                block = jnp.concatenate(
                    [rs[s, t, pl.ds(y, channels, stride=SUB), :] for s in range(4)], axis=0
                )
                t4[h, t * LANES : (t + 1) * LANES, :] = block.T
        for h in range(ROW_UNROLL):
            y = i * ROW_UNROLL + h
            lhs = jnp.concatenate(
                [t4[h, begin : begin + rows_out, :], t4[h, begin + 4 : begin + 4 + rows_out, :]],
                axis=1,
            ).astype(jnp.bfloat16)
            l_row = jnp.concatenate(
                [lf[t, pl.ds(y, channels, stride=SUB), :] for t in range(2)], axis=1
            ).astype(jnp.bfloat16)
            rhs = jnp.concatenate([l_row] * 8, axis=0) * keep
            scores = jnp.dot(lhs, rhs, preferred_element_type=jnp.float32)
            for t in range(2):
                x = scores[LANES * t : LANES * t + D + LANES - 8, LANES * t : LANES * (t + 1)]
                for bit in (64, 32, 16, 8):
                    size = x.shape[0] - bit
                    on = (iota((size, LANES), 1) // bit) % 2 == 1
                    x = jnp.where(on, x[bit:], x[:size])
                u[t, pl.ds(pl.multiple_of(y * PITCH, 8), D), :] = x
        return carry

    lax.fori_loop(0, SUB // ROW_UNROLL, row, 0)

    scale = LOG2E / math.sqrt(channels)
    reach = offs_ref[0] * tile
    half = [usable[:, :LANES], usable[:, LANES:]]
    none = jnp.zeros((SUB, LANES), jnp.float32)
    for t in range(2):
        v[t, :SUB, :] = none
        v[t, (D + 1) * SUB :, :] = none
    st[:SUB, :] = none
    st[(BLOCKS + 1) * SUB :, :] = none

    def first(i, sums):
        sums = list(sums)
        for h in range(FIRST_UNROLL):
            b = i * FIRST_UNROLL + h
            planes = []
            for s in range(PER):
                j = b * PER + s
                pair = []
                for t in range(2):
                    corr = u[t, pl.ds(j, SUB, stride=PITCH), :] * scale
                    allowed = lane >= (D - 1 - j) - reach - t * LANES
                    value = jnp.where(allowed, corr, FLOOR_COST * LOG2E) * half[t]
                    v[t, pl.ds(pl.multiple_of((j + 1) * SUB, SUB), SUB), :] = value
                    e = jnp.exp2(value)
                    sums[2 * t] += e
                    sums[2 * t + 1] += e * e
                    pair.append(value)
                planes.append(pair)
            own[b] = pack(planes)
        return tuple(sums)

    sums = lax.fori_loop(0, BLOCKS // FIRST_UNROLL, first, (none,) * 4)

    place4 = (lane % GROUP) // 4
    for m in range(sent.shape[0]):
        out = own[4 * m]
        for s, (p, q) in ((1, (3, 0)), (2, (5, 2)), (3, (7, 4))):
            out = jnp.where((place4 == p) | (place4 == q), lroll(own[4 * m + s], 8 * s), out)
        sent[m] = out

    @pl.when(has_right)
    def _():
        strip_right.start()

    @pl.when(has_left)
    def _():
        strip_left.start()

    sums = lax.fori_loop(
        0, ITERS - 1, lambda i, s: step(v, st, w_ref, usable, None, s), sums
    )

    @pl.when(has_left)
    def _():
        strip_right.wait_recv()

    @pl.when(has_right)
    def _():
        strip_left.wait_recv()

    place = lane % GROUP

    def joined(m, s):
        out = jnp.where(place < 4, lroll(from_left[m], -24 - 8 * s), own[4 * m + s])
        return jnp.where(place >= 28, lroll(from_right[m], 24 - 8 * s), out)

    def over_groups(x):
        x = x + lroll(x, GROUP)
        return x + lroll(x, 2 * GROUP)

    s1, s2 = none, none
    for m in range(BLOCKS // 4):
        for s in range(4):
            value = joined(m, s)
            st[(4 * m + s + 1) * SUB : (4 * m + s + 2) * SUB, :] = value
            e = jnp.exp2(value)
            s1, s2 = s1 + e, s2 + e * e
    strip_sums = (none,) * 5
    for q in range(channels // PER):
        at = BLOCKS + q
        strip_sums = [
            a + d for a, d in zip(strip_sums, distances(joined(at // 4, at % 4)))
        ]
    strip_weights = affinity([over_groups(x) for x in strip_sums], channels)
    strip_usable = joined(mask_at // 4, mask_at % 4)
    low, high = lane < GROUP, lane >= LANES - GROUP

    def strip_step(i, sums):
        w, keep_own = coefficients(
            strip_weights, strip_usable, over_groups(sums[0]), over_groups(sums[1])
        )

        def pooled(ref, s):
            rows = three(ref, s)
            z = columns(w, *rows)
            p = z[1] + (lroll(z[0], 1) + lroll(z[2], -1))
            return p, lroll(p, GROUP), lroll(p, -GROUP), rows[1]

        def finish(b, p, up, before, down, after, value, acc):
            lower, upper = jnp.where(low, before, up), jnp.where(high, after, down)
            new = keep_own * value + ((lower + upper) + 2.0 * p)
            st[pl.ds(pl.multiple_of((b + 1) * SUB, SUB), SUB), :] = new
            e = jnp.exp2(new)
            return acc[0] + e, acc[1] + e * e

        def advance(ref, b, s, carry):
            p, up, down, before, value, acc = carry
            p_now, up_now, down_now, value_now = pooled(ref, s)
            acc = finish(b * STRIP_UNROLL + s - 1, p, up, before, down, down_now, value, acc)
            return p_now, up_now, down_now, up, value_now, acc

        def block_ref(b):
            at = pl.ds(pl.multiple_of(b * (STRIP_UNROLL * SUB), SUB), (STRIP_UNROLL + 2) * SUB)
            return st.at[at, :]

        def loop(b, carry):
            ref = block_ref(b)
            for k in range(STRIP_UNROLL):
                carry = advance(ref, b, k, carry)
            return carry

        ref = block_ref(0)
        p, up, down, value = pooled(ref, 0)
        carry = p, up, down, p, value, (none, none)
        for k in range(1, STRIP_UNROLL):
            carry = advance(ref, jnp.int32(0), k, carry)
        p, up, down, before, value, acc = lax.fori_loop(1, BLOCKS // STRIP_UNROLL, loop, carry)
        return finish(jnp.int32(BLOCKS - 1), p, up, before, down, p, value, acc)

    lax.fori_loop(0, ITERS, strip_step, (s1, s2))

    for t in range(4):
        sums_ref[t] = sums[t]

    @pl.when(has_right)
    def _():
        tile_copy.wait_send()
        strip_right.wait_send()

    @pl.when(has_left)
    def _():
        strip_left.wait_send()


def last_kernel(mask_ref, v, st, w_ref, sums_ref, disp_ref, vol_ref):
    usable = mask_ref[...].astype(jnp.float32)
    out = step(v, st, w_ref, usable, vol_ref, [sums_ref[t] for t in range(4)])
    for t in range(2):
        disp_ref[:, t * LANES : (t + 1) * LANES] = out[2 * t + 1] / out[2 * t]


def on_device(n, left_features, right_features, tile_offsets, valid_mask):
    channels, rows, tile = left_features.shape
    vmem = pl.BlockSpec(memory_space=pltpu.VMEM)
    strips = -(-(BLOCKS + channels // PER + 1) // 4) * 4
    f32 = jnp.float32
    state = pl.pallas_call(
        functools.partial(kernel, n),
        out_shape=(
            jax.ShapeDtypeStruct((2, (D + 2) * SUB, LANES), f32),
            jax.ShapeDtypeStruct(((BLOCKS + 2) * SUB, LANES), f32),
            jax.ShapeDtypeStruct((len(STEPS), SUB, tile), f32),
            jax.ShapeDtypeStruct((4, SUB, LANES), f32),
        ),
        in_specs=[vmem, vmem, pl.BlockSpec(memory_space=pltpu.SMEM), vmem],
        out_specs=(vmem,) * 4,
        scratch_shapes=[
            pltpu.VMEM((channels, rows, tile), jnp.bfloat16),
            pltpu.VMEM((2, channels * SUB, LANES), f32),
            pltpu.VMEM((4, 4, channels * SUB, LANES), f32),
            pltpu.VMEM((ROW_UNROLL, 2 * tile, LANES), f32),
            pltpu.VMEM((2, SUB * PITCH, LANES), f32),
            pltpu.VMEM((strips, SUB, LANES), f32),
            pltpu.VMEM((strips // 4, SUB, LANES), f32),
            pltpu.VMEM((strips // 4, SUB, LANES), f32),
            pltpu.VMEM((strips // 4, SUB, LANES), f32),
            pltpu.SemaphoreType.DMA((3,)),
            pltpu.SemaphoreType.DMA((3,)),
        ],
        compiler_params=pltpu.CompilerParams(
            collective_id=0, has_side_effects=True, vmem_limit_bytes=VMEM_LIMIT
        ),
    )(left_features, right_features, tile_offsets, valid_mask)
    return pl.pallas_call(
        last_kernel,
        out_shape=(
            jax.ShapeDtypeStruct((rows, tile), f32),
            jax.ShapeDtypeStruct((D, rows, tile), jnp.bfloat16),
        ),
        in_specs=[vmem] * 5,
        out_specs=(vmem, vmem),
        compiler_params=pltpu.CompilerParams(vmem_limit_bytes=VMEM_LIMIT),
    )(valid_mask, *state)


def solution(mesh):
    return jax.shard_map(
        functools.partial(on_device, mesh.shape["col"]),
        mesh=mesh,
        in_specs=(
            P(None, None, ("groups", "col")),
            P(None, None, ("groups", "col")),
            P(("groups", "col")),
            P(None, ("groups", "col")),
        ),
        out_specs=(P(None, ("groups", "col")), P(None, None, ("groups", "col"))),
        check_vma=False,
    )
```

profile of v0, /device:TPU:16, one launch (start us, length us, event | category | flops | bytes accessed | tf_op | source)
XLA Modules:
  0.0 20.5 jit_solution(1035114664671544416)
XLA Ops:
  1.3 0.0 copy-start
  1.3 0.9 %copy-done = bf16[32,8,256]{2,1,0:T(8,128)(2,1)S(1)} copy-done((bf16[32,8,256]{2,1,0:T(8,128)(2,1)S(1)}, bf16[32,8,256]{2,1,0:T(8,128)(2,1)}, u32[]{:S(2)}) %copy-start) | copy-done | bytes 131096
  2.2 0.0 copy-start.1
  2.2 0.9 %copy-done.1 = bf16[32,8,256]{2,1,0:T(8,128)(2,1)S(1)} copy-done((bf16[32,8,256]{2,1,0:T(8,128)(2,1)S(1)}, bf16[32,8,256]{2,1,0:T(8,128)(2,1)}, u32[]{:S(2)}) %copy-start.1) | copy-done | bytes 131096
  3.1 0.0 copy-start.2
  3.1 0.7 %copy-done.2 = s32[8,256]{1,0:T(8,128)S(1)} copy-done((s32[8,256]{1,0:T(8,128)S(1)}, s32[8,256]{1,0:T(8,128)}, u32[]{:S(2)}) %copy-start.2) | copy-done | bytes 8216
  3.8 14.2 %shard_map.59 = (f32[2,1552,128]{2,1,0:T(8,128)S(1)}, f32[400,128]{1,0:T(8,128)S(1)}, f32[9,8,256]{2,1,0:T(8,128)S(1)}, f32[4,8,128]{2,1,0:T(8,128)S(1)}) custom-call(bf16[32,8,256]{2,1,0:T(8,128)(2,1)S(1)} %copy-done, bf16[32,8,256]{2,1,0:T(8,128)(2,1)S(1)} %copy-done.1, s32[1]{0:T(128)S(6)} %copy.6.offs_ref, s32[8,256]{1,0:T(8,128)S(1)} %copy-done.2), custom_call_target="tpu_custom_call" | custom-call | tf_op jit(solution)/shard_map/pallas_call | solution.py:466
  18.0 2.5 %shard_map.60 = (f32[8,256]{1,0:T(8,128)}, bf16[192,8,256]{2,1,0:T(8,128)(2,1)}) custom-call(s32[8,256]{1,0:T(8,128)S(1)} %copy-done.2, f32[2,1552,128]{2,1,0:T(8,128)S(1)} %get-tuple-element.6.v, f32[400,128]{1,0:T(8,128)S(1)} %get-tuple-element.7.st, f32[9,8,256]{2,1,0:T(8,128)S(1)} %get-tuple-element.8.w_ref, f32[4,8,128]{2,1,0:T(8,128)S(1)} %get-tuple-element.9.sums_ref), custom_call_target="tpu_custom_call" | custom-call | tf_op jit(solution)/shard_map/pallas_call | solution.py:493
Async XLA Ops:
  1.3 0.9 %copy-start = (bf16[32,8,256]{2,1,0:T(8,128)(2,1)S(1)}, bf16[32,8,256]{2,1,0:T(8,128)(2,1)}, u32[]{:S(2)}) copy-start(bf16[32,8,256]{2,1,0:T(8,128)(2,1)} %left_ref.1) | copy-start | bytes 393220
  2.2 0.9 %copy-start.1 = (bf16[32,8,256]{2,1,0:T(8,128)(2,1)S(1)}, bf16[32,8,256]{2,1,0:T(8,128)(2,1)}, u32[]{:S(2)}) copy-start(bf16[32,8,256]{2,1,0:T(8,128)(2,1)} %right_ref.1) | copy-start | bytes 393220
  3.1 0.7 %copy-start.2 = (s32[8,256]{1,0:T(8,128)S(1)}, s32[8,256]{1,0:T(8,128)}, u32[]{:S(2)}) copy-start(s32[8,256]{1,0:T(8,128)} %mask_ref.3) | copy-start | bytes 24580
where the time goes:
time: 20.7 us; the launch traced here: 20.5 us
  Pallas kernels  16.7 us (81%)
  local copies, waits for them, and re-layouts  2.5 us (12%)
  between operations  1.29 us (6%)
    pallas_call x1, Pallas kernels, on_device(): pl.pallas_call(functools.partial(kernel, n), out_shape=(jax.ShapeDtypeStr...  14.2 us
    pallas_call x1, Pallas kernels, on_device(): pl.pallas_call(last_kernel, out_shape=(jax.ShapeDtypeStruct((rows, tile),...  2.51 us
    unnamed x6, local copies, waits for them, and re-layouts  2.5 us

commit v1 on v0

--- a/solution.py
+++ b/solution.py
@@ -22,8 +22,8 @@
 LOG2E = math.log2(math.e)
 FIRST_UNROLL = 48
 UNROLL = 192
+PUT = 48
 STRIP_UNROLL = 48
-ROW_UNROLL = 8
 CHANNEL_UNROLL = 32
 VMEM_LIMIT = 24 * 1024 * 1024
 
@@ -93,7 +93,7 @@
     return out
 
 
-def step(v, st, w_ref, usable, vol_ref, sums):
+def step(v, st, w_ref, usable, vol_ref, sums, done=None):
     last = vol_ref is not None
     lane = iota((SUB, LANES), 1)
     head_lane, tail_lane = lane == 0, lane == LANES - 1
@@ -130,6 +130,7 @@
             pair[1] = jnp.where(lane >= LANES - 4, lroll(strip, 100 - GROUP * group), pair[1])
             out = jnp.concatenate(pair, axis=1) * (1.0 / LOG2E)
             vol_ref[D - 1 - j] = out.astype(jnp.bfloat16)
+            done(b * UNROLL + s if isinstance(b, int) else s)
             level = (D - 1 - j).astype(jnp.float32) * (1.0 / D)
         for t in range(2):
             if not last:
@@ -171,8 +172,9 @@
 
 
 def kernel(
-    n, left_ref, right_ref, offs_ref, mask_ref, v, st, w_ref, sums_ref,
-    prev, lf, rs, t4, u, own, sent, from_left, from_right, send_sem, recv_sem,
+    n, left_hbm, right_hbm, offs_hbm, mask_hbm, v, st, w_ref, sums_ref, usable_ref,
+    left_ref, right_ref, mask_ref, offs_ref,
+    prev, lf, rs, t4, part, u, own, sent, from_left, from_right, load_sem, send_sem, recv_sem,
 ):
     channels = left_ref.shape[0]
     tile = left_ref.shape[2]
@@ -182,15 +184,31 @@
 
     barrier = pltpu.get_barrier_semaphore()
 
+    @pl.when(has_right)
+    def _():
+        pl.semaphore_signal(barrier, inc=1, device_id={"col": me + 1}, device_id_type=MESH)
+
     @pl.when(has_left)
     def _():
         pl.semaphore_signal(barrier, inc=1, device_id={"col": me - 1}, device_id_type=MESH)
 
-    @pl.when(has_right)
-    def _():
-        pl.semaphore_signal(barrier, inc=1, device_id={"col": me + 1}, device_id_type=MESH)
-
-    pl.semaphore_wait(barrier, has_left.astype(jnp.int32) + has_right.astype(jnp.int32))
+    loads = [
+        pltpu.make_async_copy(src, dst, load_sem.at[i])
+        for i, (src, dst) in enumerate((
+            (left_hbm, left_ref), (right_hbm, right_ref), (mask_hbm, mask_ref), (offs_hbm, offs_ref)
+        ))
+    ]
+    for load in loads:
+        load.start()
+
+    @pl.when(jnp.logical_not(has_left))
+    def _():
+        prev[...] = jnp.zeros(prev.shape, prev.dtype)
+        from_left[...] = jnp.zeros(from_left.shape, jnp.float32)
+
+    @pl.when(jnp.logical_not(has_right))
+    def _():
+        from_right[...] = jnp.zeros(from_right.shape, jnp.float32)
 
     def remote(src, dst, slot, to):
         return pltpu.make_async_remote_copy(
@@ -198,24 +216,26 @@
             device_id={"col": to}, device_id_type=MESH,
         )
 
-    tile_copy = remote(right_ref, prev, 0, me + 1)
-    strip_right = remote(sent, from_left, 1, me + 1)
-    strip_left = remote(sent, from_right, 2, me - 1)
+    halves = [pl.ds(t * LANES, LANES) for t in range(tile // LANES)]
+    tile_copies = [
+        remote(right_hbm.at[:, :, half], prev.at[:, :, half], 2 + t, me + 1)
+        for t, half in enumerate(halves)
+    ]
+    strip_right = remote(sent, from_left, 0, me + 1)
+    strip_left = remote(sent, from_right, 1, me - 1)
+
+    pl.semaphore_wait(barrier, has_left.astype(jnp.int32) + has_right.astype(jnp.int32))
 
     @pl.when(has_right)
     def _():
-        tile_copy.start()
-
-    @pl.when(jnp.logical_not(has_left))
-    def _():
-        prev[...] = jnp.zeros(prev.shape, prev.dtype)
-        from_left[...] = jnp.zeros(from_left.shape, jnp.float32)
-
-    @pl.when(jnp.logical_not(has_right))
-    def _():
-        from_right[...] = jnp.zeros(from_right.shape, jnp.float32)
+        for copy in tile_copies[::-1]:
+            copy.start()
+
+    for load in (loads[0], loads[2]):
+        load.wait()
 
     usable = mask_ref[...].astype(jnp.float32)
+    usable_ref[...] = usable
 
     zero = jnp.zeros((SUB, tile), jnp.float32)
 
@@ -252,61 +272,74 @@
     for q in range(mask_at + 1, own.shape[0]):
         own[q] = jnp.zeros((SUB, LANES), jnp.float32)
 
-    @pl.when(has_left)
-    def _():
-        tile_copy.wait_recv()
-
-    def shifts(c, carry):
-        at = pl.ds(pl.multiple_of(c * SUB, SUB), SUB)
-        before = prev[c].astype(jnp.float32)
-        mine = right_ref[c].astype(jnp.float32)
-        parts = (before[:, :LANES], before[:, LANES:], mine[:, :LANES], mine[:, LANES:])
-        for s in range(4):
-            rolled = [lroll(p, -s) for p in parts]
-            for t in range(4):
-                value = rolled[t]
-                if s and t < 3:
-                    value = jnp.where(lane < LANES - s, value, rolled[t + 1])
-                rs[s, t, at, :] = value
-        return carry
-
-    lax.fori_loop(0, channels // per, unrolled(shifts), 0)
+    loads[1].wait()
+
+    def shifts(source, first, extra):
+        def run(c, carry):
+            at = pl.ds(pl.multiple_of(c * SUB, SUB), SUB)
+            parts = [source[c, :, t * LANES : (t + 1) * LANES].astype(jnp.float32) for t in range(2)]
+            if extra is not None:
+                parts.append(extra[c, :, :LANES].astype(jnp.float32))
+            for s in range(4):
+                rolled = [lroll(p, -s) for p in parts]
+                for t in range(2):
+                    value = rolled[t]
+                    if s and t + 1 < len(parts):
+                        value = jnp.where(lane < LANES - s, value, rolled[t + 1])
+                    rs[s, first + t, at, :] = value
+            return carry
+
+        return run
 
     depth = 8 * channels
     keep = (iota((depth, tile), 0) // channels == iota((depth, tile), 1) % 8).astype(jnp.bfloat16)
     rows_out = tile - 8 + D
     begin = tile - D + 1
-
-    def row(i, carry):
-        for h in range(ROW_UNROLL):
-            y = i * ROW_UNROLL + h
-            for t in range(4):
-                block = jnp.concatenate(
-                    [rs[s, t, pl.ds(y, channels, stride=SUB), :] for s in range(4)], axis=0
-                )
-                t4[h, t * LANES : (t + 1) * LANES, :] = block.T
-        for h in range(ROW_UNROLL):
-            y = i * ROW_UNROLL + h
-            lhs = jnp.concatenate(
-                [t4[h, begin : begin + rows_out, :], t4[h, begin + 4 : begin + 4 + rows_out, :]],
-                axis=1,
-            ).astype(jnp.bfloat16)
-            l_row = jnp.concatenate(
-                [lf[t, pl.ds(y, channels, stride=SUB), :] for t in range(2)], axis=1
-            ).astype(jnp.bfloat16)
-            rhs = jnp.concatenate([l_row] * 8, axis=0) * keep
-            scores = jnp.dot(lhs, rhs, preferred_element_type=jnp.float32)
-            for t in range(2):
-                x = scores[LANES * t : LANES * t + D + LANES - 8, LANES * t : LANES * (t + 1)]
-                for bit in (64, 32, 16, 8):
-                    size = x.shape[0] - bit
-                    on = (iota((size, LANES), 1) // bit) % 2 == 1
-                    x = jnp.where(on, x[bit:], x[:size])
-                u[t, pl.ds(pl.multiple_of(y * PITCH, 8), D), :] = x
-        return carry
-
-    lax.fori_loop(0, SUB // ROW_UNROLL, row, 0)
-
+    cut = D
+
+    def transposes(y, tiles):
+        for t in tiles:
+            block = jnp.concatenate(
+                [rs[s, t, pl.ds(y, channels, stride=SUB), :] for s in range(4)], axis=0
+            )
+            t4[y, t * LANES : (t + 1) * LANES, :] = block.T
+
+    def scores_of(y, low, high):
+        lhs = jnp.concatenate(
+            [t4[y, begin + low : begin + high, :], t4[y, begin + 4 + low : begin + 4 + high, :]],
+            axis=1,
+        ).astype(jnp.bfloat16)
+        l_row = jnp.concatenate(
+            [lf[t, pl.ds(y, channels, stride=SUB), :] for t in range(2)], axis=1
+        ).astype(jnp.bfloat16)
+        rhs = jnp.concatenate([l_row] * 8, axis=0) * keep
+        return jnp.dot(lhs, rhs, preferred_element_type=jnp.float32)
+
+    lax.fori_loop(0, channels // per, unrolled(shifts(right_ref, 2, None)), 0)
+    for y in range(SUB):
+        transposes(y, (2, 3))
+    for y in range(SUB):
+        part[y] = scores_of(y, cut, rows_out)
+
+    @pl.when(has_left)
+    def _():
+        for copy in tile_copies[::-1]:
+            copy.wait_recv()
+
+    lax.fori_loop(0, channels // per, unrolled(shifts(prev, 0, right_ref)), 0)
+    for y in range(SUB):
+        transposes(y, (0, 1))
+    for y in range(SUB):
+        scores = jnp.concatenate([scores_of(y, 0, cut), part[y]], axis=0)
+        for t in range(2):
+            x = scores[LANES * t : LANES * t + D + LANES - 8, LANES * t : LANES * (t + 1)]
+            for bit in (64, 32, 16, 8):
+                size = x.shape[0] - bit
+                on = (iota((size, LANES), 1) // bit) % 2 == 1
+                x = jnp.where(on, x[bit:], x[:size])
+            u[t, y * PITCH : y * PITCH + D, :] = x
+
+    loads[3].wait()
     scale = LOG2E / math.sqrt(channels)
     reach = offs_ref[0] * tile
     half = [usable[:, :LANES], usable[:, LANES:]]
@@ -443,7 +476,8 @@
 
     @pl.when(has_right)
     def _():
-        tile_copy.wait_send()
+        for copy in tile_copies:
+            copy.wait_send()
         strip_right.wait_send()
 
     @pl.when(has_left)
@@ -451,16 +485,29 @@
         strip_left.wait_send()
 
 
-def last_kernel(mask_ref, v, st, w_ref, sums_ref, disp_ref, vol_ref):
-    usable = mask_ref[...].astype(jnp.float32)
-    out = step(v, st, w_ref, usable, vol_ref, [sums_ref[t] for t in range(4)])
+def last_kernel(usable_ref, v, st, w_ref, sums_ref, disp_hbm, vol_hbm, disp_ref, vol_ref, sem):
+    def put(b):
+        at = pl.ds(D - (b + 1) * PUT, PUT)
+        return pltpu.make_async_copy(vol_ref.at[at], vol_hbm.at[at], sem.at[b])
+
+    def done(j):
+        if (j + 1) % PUT == 0:
+            put(j // PUT).start()
+
+    out = step(v, st, w_ref, usable_ref[...], vol_ref, [sums_ref[t] for t in range(4)], done)
     for t in range(2):
         disp_ref[:, t * LANES : (t + 1) * LANES] = out[2 * t + 1] / out[2 * t]
+    disp = pltpu.make_async_copy(disp_ref, disp_hbm, sem.at[D // PUT])
+    disp.start()
+    for b in range(D // PUT):
+        put(b).wait()
+    disp.wait()
 
 
 def on_device(n, left_features, right_features, tile_offsets, valid_mask):
     channels, rows, tile = left_features.shape
     vmem = pl.BlockSpec(memory_space=pltpu.VMEM)
+    hbm = pl.BlockSpec(memory_space=pltpu.HBM)
     strips = -(-(BLOCKS + channels // PER + 1) // 4) * 4
     f32 = jnp.float32
     state = pl.pallas_call(
@@ -470,26 +517,34 @@
             jax.ShapeDtypeStruct(((BLOCKS + 2) * SUB, LANES), f32),
             jax.ShapeDtypeStruct((len(STEPS), SUB, tile), f32),
             jax.ShapeDtypeStruct((4, SUB, LANES), f32),
+            jax.ShapeDtypeStruct((SUB, tile), f32),
         ),
-        in_specs=[vmem, vmem, pl.BlockSpec(memory_space=pltpu.SMEM), vmem],
-        out_specs=(vmem,) * 4,
+        in_specs=[hbm] * 4,
+        out_specs=(vmem,) * 5,
         scratch_shapes=[
+            pltpu.VMEM((channels, rows, tile), jnp.bfloat16),
+            pltpu.VMEM((channels, rows, tile), jnp.bfloat16),
+            pltpu.VMEM((rows, tile), jnp.int32),
+            pltpu.SMEM((1,), jnp.int32),
             pltpu.VMEM((channels, rows, tile), jnp.bfloat16),
             pltpu.VMEM((2, channels * SUB, LANES), f32),
             pltpu.VMEM((4, 4, channels * SUB, LANES), f32),
-            pltpu.VMEM((ROW_UNROLL, 2 * tile, LANES), f32),
+            pltpu.VMEM((SUB, 2 * tile, LANES), f32),
+            pltpu.VMEM((SUB, tile - 8, tile), f32),
             pltpu.VMEM((2, SUB * PITCH, LANES), f32),
             pltpu.VMEM((strips, SUB, LANES), f32),
             pltpu.VMEM((strips // 4, SUB, LANES), f32),
             pltpu.VMEM((strips // 4, SUB, LANES), f32),
             pltpu.VMEM((strips // 4, SUB, LANES), f32),
-            pltpu.SemaphoreType.DMA((3,)),
-            pltpu.SemaphoreType.DMA((3,)),
+            pltpu.SemaphoreType.DMA((4,)),
+            pltpu.SemaphoreType.DMA((4,)),
+            pltpu.SemaphoreType.DMA((4,)),
         ],
         compiler_params=pltpu.CompilerParams(
             collective_id=0, has_side_effects=True, vmem_limit_bytes=VMEM_LIMIT
         ),
     )(left_features, right_features, tile_offsets, valid_mask)
+    v, st, w, sums, usable = state
     return pl.pallas_call(
         last_kernel,
         out_shape=(
@@ -497,9 +552,14 @@
             jax.ShapeDtypeStruct((D, rows, tile), jnp.bfloat16),
         ),
         in_specs=[vmem] * 5,
-        out_specs=(vmem, vmem),
+        out_specs=(hbm, hbm),
+        scratch_shapes=[
+            pltpu.VMEM((rows, tile), f32),
+            pltpu.VMEM((D, rows, tile), jnp.bfloat16),
+            pltpu.SemaphoreType.DMA((D // PUT + 1,)),
+        ],
         compiler_params=pltpu.CompilerParams(vmem_limit_bytes=VMEM_LIMIT),
-    )(valid_mask, *state)
+    )(usable, v, st, w, sums)
 
 
 def solution(mesh):

time: 20.7 us -> 20 us (0.966)
  Pallas kernels: 16.7 us -> 16 us
    pallas_call x1, Pallas kernels: 14.2 us -> 13.7 us  [on_device(): pl.pallas_call(functools.partial(kernel, n), out_shape=(jax.ShapeDtypeStr...]
where the time goes in v1:
time: 20 us; the launch traced here: 19.8 us
  Pallas kernels  16 us (80%)
  local copies, waits for them, and re-layouts  2.5 us (12%)
  between operations  1.29 us (6%)
    pallas_call x1, Pallas kernels, on_device(): pl.pallas_call(functools.partial(kernel, n), out_shape=(jax.ShapeDtypeStr...  13.7 us
    unnamed x6, local copies, waits for them, and re-layouts  2.5 us
    pallas_call x1, Pallas kernels, on_device(): pl.pallas_call(last_kernel, out_shape=(jax.ShapeDtypeStruct((rows, tile),...  2.32 us

profile of v1, /device:TPU:16, one launch (start us, length us, event | category | flops | bytes accessed | tf_op | source)
XLA Modules:
  0.0 19.8 jit_solution(5829643143364131742)
XLA Ops:
  1.3 0.0 copy-start
  1.3 0.9 %copy-done = bf16[32,8,256]{2,1,0:T(8,128)(2,1)S(1)} copy-done((bf16[32,8,256]{2,1,0:T(8,128)(2,1)S(1)}, bf16[32,8,256]{2,1,0:T(8,128)(2,1)}, u32[]{:S(2)}) %copy-start) | copy-done | bytes 131096
  2.2 0.0 copy-start.1
  2.2 0.9 %copy-done.1 = bf16[32,8,256]{2,1,0:T(8,128)(2,1)S(1)} copy-done((bf16[32,8,256]{2,1,0:T(8,128)(2,1)S(1)}, bf16[32,8,256]{2,1,0:T(8,128)(2,1)}, u32[]{:S(2)}) %copy-start.1) | copy-done | bytes 131096
  3.1 0.0 copy-start.2
  3.1 0.7 %copy-done.2 = s32[8,256]{1,0:T(8,128)S(1)} copy-done((s32[8,256]{1,0:T(8,128)S(1)}, s32[8,256]{1,0:T(8,128)}, u32[]{:S(2)}) %copy-start.2) | copy-done | bytes 8216
  3.8 13.7 %shard_map.59 = (f32[2,1552,128]{2,1,0:T(8,128)S(1)}, f32[400,128]{1,0:T(8,128)S(1)}, f32[9,8,256]{2,1,0:T(8,128)S(1)}, f32[4,8,128]{2,1,0:T(8,128)S(1)}, f32[8,256]{1,0:T(8,128)S(1)}) custom-call(bf16[32,8,256]{2,1,0:T(8,128)(2,1)S(1)} %copy-done, bf16[32,8,256]{2,1,0:T(8,128)(2,1)S(1)} %copy-done.1, s32[1]{0:T(128)S(6)} %copy.6.offs_hbm, ...), custom_call_target="tpu_custom_call" | custom-call | tf_op jit(solution)/shard_map/pallas_call | solution.py:513
  17.5 2.3 %shard_map.60 = (f32[8,256]{1,0:T(8,128)}, bf16[192,8,256]{2,1,0:T(8,128)(2,1)}) custom-call(f32[8,256]{1,0:T(8,128)S(1)} %get-tuple-element.7.usable_ref, f32[2,1552,128]{2,1,0:T(8,128)S(1)} %get-tuple-element.8.v, f32[400,128]{1,0:T(8,128)S(1)} %get-tuple-element.9.st, f32[9,8,256]{2,1,0:T(8,128)S(1)} %get-tuple-element.10.w_ref, ...), custom_call_target="tpu_custom_call" | custom-call | tf_op jit(solution)/shard_map/pallas_call | solution.py:548
Async XLA Ops:
  1.3 0.9 %copy-start = (bf16[32,8,256]{2,1,0:T(8,128)(2,1)S(1)}, bf16[32,8,256]{2,1,0:T(8,128)(2,1)}, u32[]{:S(2)}) copy-start(bf16[32,8,256]{2,1,0:T(8,128)(2,1)} %left_hbm.1) | copy-start | bytes 393220
  2.2 0.9 %copy-start.1 = (bf16[32,8,256]{2,1,0:T(8,128)(2,1)S(1)}, bf16[32,8,256]{2,1,0:T(8,128)(2,1)}, u32[]{:S(2)}) copy-start(bf16[32,8,256]{2,1,0:T(8,128)(2,1)} %right_hbm.1) | copy-start | bytes 393220
  3.1 0.7 %copy-start.2 = (s32[8,256]{1,0:T(8,128)S(1)}, s32[8,256]{1,0:T(8,128)}, u32[]{:S(2)}) copy-start(s32[8,256]{1,0:T(8,128)} %mask_hbm.1) | copy-start | bytes 24580

commit v2 on v1

--- a/solution.py
+++ b/solution.py
@@ -172,8 +172,8 @@
 
 
 def kernel(
-    n, left_hbm, right_hbm, offs_hbm, mask_hbm, v, st, w_ref, sums_ref, usable_ref,
-    left_ref, right_ref, mask_ref, offs_ref,
+    n, left_hbm, right_hbm, mask_hbm, offs_ref, v, st, w_ref, sums_ref, usable_ref,
+    left_ref, right_ref, mask_ref,
     prev, lf, rs, t4, part, u, own, sent, from_left, from_right, load_sem, send_sem, recv_sem,
 ):
     channels = left_ref.shape[0]
@@ -195,7 +195,7 @@
     loads = [
         pltpu.make_async_copy(src, dst, load_sem.at[i])
         for i, (src, dst) in enumerate((
-            (left_hbm, left_ref), (right_hbm, right_ref), (mask_hbm, mask_ref), (offs_hbm, offs_ref)
+            (left_hbm, left_ref), (right_hbm, right_ref), (mask_hbm, mask_ref)
         ))
     ]
     for load in loads:
@@ -339,7 +339,6 @@
                 x = jnp.where(on, x[bit:], x[:size])
             u[t, y * PITCH : y * PITCH + D, :] = x
 
-    loads[3].wait()
     scale = LOG2E / math.sqrt(channels)
     reach = offs_ref[0] * tile
     half = [usable[:, :LANES], usable[:, LANES:]]
@@ -519,13 +518,12 @@
             jax.ShapeDtypeStruct((4, SUB, LANES), f32),
             jax.ShapeDtypeStruct((SUB, tile), f32),
         ),
-        in_specs=[hbm] * 4,
+        in_specs=[hbm] * 3 + [pl.BlockSpec(memory_space=pltpu.SMEM)],
         out_specs=(vmem,) * 5,
         scratch_shapes=[
             pltpu.VMEM((channels, rows, tile), jnp.bfloat16),
             pltpu.VMEM((channels, rows, tile), jnp.bfloat16),
             pltpu.VMEM((rows, tile), jnp.int32),
-            pltpu.SMEM((1,), jnp.int32),
             pltpu.VMEM((channels, rows, tile), jnp.bfloat16),
             pltpu.VMEM((2, channels * SUB, LANES), f32),
             pltpu.VMEM((4, 4, channels * SUB, LANES), f32),
@@ -536,14 +534,17 @@
             pltpu.VMEM((strips // 4, SUB, LANES), f32),
             pltpu.VMEM((strips // 4, SUB, LANES), f32),
             pltpu.VMEM((strips // 4, SUB, LANES), f32),
-            pltpu.SemaphoreType.DMA((4,)),
+            pltpu.SemaphoreType.DMA((3,)),
             pltpu.SemaphoreType.DMA((4,)),
             pltpu.SemaphoreType.DMA((4,)),
         ],
         compiler_params=pltpu.CompilerParams(
             collective_id=0, has_side_effects=True, vmem_limit_bytes=VMEM_LIMIT
         ),
-    )(left_features, right_features, tile_offsets, valid_mask)
+    )(
+        *(pltpu.with_memory_space_constraint(x, pltpu.HBM) for x in (left_features, right_features, valid_mask)),
+        tile_offsets,
+    )
     v, st, w, sums, usable = state
     return pl.pallas_call(
         last_kernel,

time: 20 us -> 17.7 us (0.89)
  local copies, waits for them, and re-layouts: 2.5 us -> 0 us
  Pallas kernels: 16 us -> 16.3 us
    unnamed x6 -> x0, local copies, waits for them, and re-layouts: 2.5 us -> none
    pallas_call x1, Pallas kernels: 13.7 us -> 14 us  [on_device(): pl.pallas_call(functools.partial(kernel, n), out_shape=(jax.ShapeDtypeStr...]
where the time goes in v2:
time: 17.7 us; the launch traced here: 17.5 us
  Pallas kernels  16.3 us (92%)
  between operations  1.28 us (7%)
    pallas_call x1, Pallas kernels, on_device(): pl.pallas_call(functools.partial(kernel, n), out_shape=(jax.ShapeDtypeStr...  14 us
    pallas_call x1, Pallas kernels, on_device(): pl.pallas_call(last_kernel, out_shape=(jax.ShapeDtypeStruct((rows, tile),...  2.3 us

profile of v2, /device:TPU:16, one launch (start us, length us, event | category | flops | bytes accessed | tf_op | source)
XLA Modules:
  0.0 17.5 jit_solution(7172592460797970017)
XLA Ops:
  1.3 14.0 %shard_map.59 = (f32[2,1552,128]{2,1,0:T(8,128)S(1)}, f32[400,128]{1,0:T(8,128)S(1)}, f32[9,8,256]{2,1,0:T(8,128)S(1)}, f32[4,8,128]{2,1,0:T(8,128)S(1)}, f32[8,256]{1,0:T(8,128)S(1)}) custom-call(bf16[32,8,256]{2,1,0:T(8,128)(2,1)} %left_hbm.1, bf16[32,8,256]{2,1,0:T(8,128)(2,1)} %right_hbm.1, s32[8,256]{1,0:T(8,128)} %mask_hbm.1, s32[1]{0:T(128)S(6)} %copy.6.offs_ref), custom_call_target="tpu_custom_call" | custom-call | tf_op jit(solution)/shard_map/pallas_call | solution.py:512
  15.2 2.3 %shard_map.60 = (f32[8,256]{1,0:T(8,128)}, bf16[192,8,256]{2,1,0:T(8,128)(2,1)}) custom-call(f32[8,256]{1,0:T(8,128)S(1)} %get-tuple-element.7.usable_ref, f32[2,1552,128]{2,1,0:T(8,128)S(1)} %get-tuple-element.8.v, f32[400,128]{1,0:T(8,128)S(1)} %get-tuple-element.9.st, f32[9,8,256]{2,1,0:T(8,128)S(1)} %get-tuple-element.10.w_ref, ...), custom_call_target="tpu_custom_call" | custom-call | tf_op jit(solution)/shard_map/pallas_call | solution.py:549

commit v3 on v2

--- a/solution.py
+++ b/solution.py
@@ -22,8 +22,7 @@
 LOG2E = math.log2(math.e)
 FIRST_UNROLL = 48
 UNROLL = 192
-PUT = 48
-STRIP_UNROLL = 48
+PUT = 16
 CHANNEL_UNROLL = 32
 VMEM_LIMIT = 24 * 1024 * 1024
 
@@ -123,9 +122,8 @@
         j = b * UNROLL + s
         pair, sums = list(pair), list(sums)
         if last:
-            group = s % PER
-            row = pl.multiple_of((b * (UNROLL // PER) + s // PER + 1) * SUB, SUB)
-            strip = st[pl.ds(row, SUB), :]
+            group = s // BLOCKS
+            strip = st[(s % BLOCKS + 1) * SUB : (s % BLOCKS + 2) * SUB, :]
             pair[0] = jnp.where(lane < 4, lroll(strip, -(GROUP * group + 4)), pair[0])
             pair[1] = jnp.where(lane >= LANES - 4, lroll(strip, 100 - GROUP * group), pair[1])
             out = jnp.concatenate(pair, axis=1) * (1.0 / LOG2E)
@@ -174,7 +172,7 @@
 def kernel(
     n, left_hbm, right_hbm, mask_hbm, offs_ref, v, st, w_ref, sums_ref, usable_ref,
     left_ref, right_ref, mask_ref,
-    prev, lf, rs, t4, part, u, own, sent, from_left, from_right, load_sem, send_sem, recv_sem,
+    high, low_out, low_in, lf, rs, t4, rhs_ref, part, u, own, sent, from_left, from_right, load_sem, send_sem, recv_sem,
 ):
     channels = left_ref.shape[0]
     tile = left_ref.shape[2]
@@ -203,7 +201,8 @@
 
     @pl.when(jnp.logical_not(has_left))
     def _():
-        prev[...] = jnp.zeros(prev.shape, prev.dtype)
+        high[...] = jnp.zeros(high.shape, high.dtype)
+        low_in[...] = jnp.zeros(low_in.shape, low_in.dtype)
         from_left[...] = jnp.zeros(from_left.shape, jnp.float32)
 
     @pl.when(jnp.logical_not(has_right))
@@ -216,11 +215,8 @@
             device_id={"col": to}, device_id_type=MESH,
         )
 
-    halves = [pl.ds(t * LANES, LANES) for t in range(tile // LANES)]
-    tile_copies = [
-        remote(right_hbm.at[:, :, half], prev.at[:, :, half], 2 + t, me + 1)
-        for t, half in enumerate(halves)
-    ]
+    high_copy = remote(right_hbm.at[:, :, pl.ds(LANES, LANES)], high, 2, me + 1)
+    low_copy = remote(low_out, low_in, 3, me + 1)
     strip_right = remote(sent, from_left, 0, me + 1)
     strip_left = remote(sent, from_right, 1, me - 1)
 
@@ -228,8 +224,14 @@
 
     @pl.when(has_right)
     def _():
-        for copy in tile_copies[::-1]:
-            copy.start()
+        high_copy.start()
+
+    loads[1].wait()
+    half = channels // 2
+    for c in range(half):
+        lead = right_ref[c, :, :LANES].astype(jnp.float32)
+        trail = right_ref[c + half, :, :LANES].astype(jnp.float32)
+        low_out[c] = jnp.where(lane < LANES // 2, lroll(lead, LANES // 2), trail).astype(low_out.dtype)
 
     for load in (loads[0], loads[2]):
         load.wait()
@@ -267,77 +269,90 @@
             for s in range(PER)
         ]
         own[BLOCKS + q] = pack(planes)
+    @pl.when(has_right)
+    def _():
+        low_copy.start()
+
     mask_at = BLOCKS + channels // PER
     own[mask_at] = pack([(usable[:, :LANES], usable[:, LANES:])] * PER)
     for q in range(mask_at + 1, own.shape[0]):
         own[q] = jnp.zeros((SUB, LANES), jnp.float32)
 
-    loads[1].wait()
-
-    def shifts(source, first, extra):
-        def run(c, carry):
-            at = pl.ds(pl.multiple_of(c * SUB, SUB), SUB)
-            parts = [source[c, :, t * LANES : (t + 1) * LANES].astype(jnp.float32) for t in range(2)]
-            if extra is not None:
-                parts.append(extra[c, :, :LANES].astype(jnp.float32))
+    def own_part(t):
+        return lambda c: right_ref[c, :, t * LANES : (t + 1) * LANES].astype(jnp.float32)
+
+    def high_part(c):
+        return high[c].astype(jnp.float32)
+
+    def low_part(c):
+        x = low_in[c % half].astype(jnp.float32)
+        return lroll(x, LANES // 2) if c < half else x
+
+    def shifts(t, part_of, next_of):
+        for c in range(channels):
+            now = part_of(c)
+            after = now if next_of is None else next_of(c)
             for s in range(4):
-                rolled = [lroll(p, -s) for p in parts]
-                for t in range(2):
-                    value = rolled[t]
-                    if s and t + 1 < len(parts):
-                        value = jnp.where(lane < LANES - s, value, rolled[t + 1])
-                    rs[s, first + t, at, :] = value
-            return carry
-
-        return run
+                value = lroll(jnp.where(lane < s, after, now), -s) if s else now
+                rs[s, t, c * SUB : (c + 1) * SUB, :] = value
 
     depth = 8 * channels
     keep = (iota((depth, tile), 0) // channels == iota((depth, tile), 1) % 8).astype(jnp.bfloat16)
     rows_out = tile - 8 + D
     begin = tile - D + 1
-    cut = D
-
-    def transposes(y, tiles):
-        for t in tiles:
+    first_cut, second_cut = LANES // 2, D
+
+    def transposes(t):
+        for y in range(SUB):
             block = jnp.concatenate(
                 [rs[s, t, pl.ds(y, channels, stride=SUB), :] for s in range(4)], axis=0
             )
             t4[y, t * LANES : (t + 1) * LANES, :] = block.T
 
-    def scores_of(y, low, high):
+    def scores_of(y, low, high, width):
         lhs = jnp.concatenate(
             [t4[y, begin + low : begin + high, :], t4[y, begin + 4 + low : begin + 4 + high, :]],
             axis=1,
         ).astype(jnp.bfloat16)
+        return jnp.dot(lhs, rhs_ref[y, :, :width], preferred_element_type=jnp.float32)
+
+    def straighten(y, t, x):
+        for bit in (64, 32, 16, 8):
+            size = x.shape[0] - bit
+            on = (iota((size, LANES), 1) // bit) % 2 == 1
+            x = jnp.where(on, x[bit:], x[:size])
+        u[t, y * PITCH : y * PITCH + D, :] = x
+
+    shifts(2, own_part(0), own_part(1))
+    shifts(3, own_part(1), None)
+    transposes(2)
+    transposes(3)
+    for y in range(SUB):
         l_row = jnp.concatenate(
             [lf[t, pl.ds(y, channels, stride=SUB), :] for t in range(2)], axis=1
         ).astype(jnp.bfloat16)
-        rhs = jnp.concatenate([l_row] * 8, axis=0) * keep
-        return jnp.dot(lhs, rhs, preferred_element_type=jnp.float32)
-
-    lax.fori_loop(0, channels // per, unrolled(shifts(right_ref, 2, None)), 0)
+        rhs_ref[y] = jnp.concatenate([l_row] * 8, axis=0) * keep
+        part[y, second_cut:, :] = scores_of(y, second_cut, rows_out, tile)
+
+    @pl.when(has_left)
+    def _():
+        high_copy.wait_recv()
+
+    shifts(1, high_part, own_part(0))
+    transposes(1)
     for y in range(SUB):
-        transposes(y, (2, 3))
+        part[y, first_cut:second_cut, :] = scores_of(y, first_cut, second_cut, tile)
+        straighten(y, 1, part[y, LANES:, LANES:])
+
+    @pl.when(has_left)
+    def _():
+        low_copy.wait_recv()
+
+    shifts(0, low_part, high_part)
+    transposes(0)
     for y in range(SUB):
-        part[y] = scores_of(y, cut, rows_out)
-
-    @pl.when(has_left)
-    def _():
-        for copy in tile_copies[::-1]:
-            copy.wait_recv()
-
-    lax.fori_loop(0, channels // per, unrolled(shifts(prev, 0, right_ref)), 0)
-    for y in range(SUB):
-        transposes(y, (0, 1))
-    for y in range(SUB):
-        scores = jnp.concatenate([scores_of(y, 0, cut), part[y]], axis=0)
-        for t in range(2):
-            x = scores[LANES * t : LANES * t + D + LANES - 8, LANES * t : LANES * (t + 1)]
-            for bit in (64, 32, 16, 8):
-                size = x.shape[0] - bit
-                on = (iota((size, LANES), 1) // bit) % 2 == 1
-                x = jnp.where(on, x[bit:], x[:size])
-            u[t, y * PITCH : y * PITCH + D, :] = x
+        x = scores_of(y, 0, first_cut, LANES)
+        straighten(y, 0, jnp.concatenate([x, part[y, first_cut : D + LANES - 8, :LANES]], axis=0))
 
     scale = LOG2E / math.sqrt(channels)
     reach = offs_ref[0] * tile
@@ -355,7 +370,7 @@
             b = i * FIRST_UNROLL + h
             planes = []
             for s in range(PER):
-                j = b * PER + s
+                j = s * BLOCKS + b
                 pair = []
                 for t in range(2):
                     corr = u[t, pl.ds(j, SUB, stride=PITCH), :] * scale
@@ -424,49 +439,37 @@
         ]
     strip_weights = affinity([over_groups(x) for x in strip_sums], channels)
     strip_usable = joined(mask_at // 4, mask_at % 4)
-    low, high = lane < GROUP, lane >= LANES - GROUP
+    lowest, highest = lane < GROUP, lane >= LANES - GROUP
 
     def strip_step(i, sums):
         w, keep_own = coefficients(
             strip_weights, strip_usable, over_groups(sums[0]), over_groups(sums[1])
         )
 
-        def pooled(ref, s):
-            rows = three(ref, s)
+        def pooled(b):
+            rows = three(st, b)
             z = columns(w, *rows)
-            p = z[1] + (lroll(z[0], 1) + lroll(z[2], -1))
-            return p, lroll(p, GROUP), lroll(p, -GROUP), rows[1]
-
-        def finish(b, p, up, before, down, after, value, acc):
-            lower, upper = jnp.where(low, before, up), jnp.where(high, after, down)
-            new = keep_own * value + ((lower + upper) + 2.0 * p)
-            st[pl.ds(pl.multiple_of((b + 1) * SUB, SUB), SUB), :] = new
+            return z[1] + (lroll(z[0], 1) + lroll(z[2], -1)), rows[1]
+
+        p, value = pooled(0)
+        p_end, value_end = pooled(BLOCKS - 1)
+        pair = p + jnp.where(lowest, p, lroll(p_end, GROUP))
+        p_after = jnp.where(highest, p_end, lroll(p, -GROUP))
+        s1, s2 = none, none
+        for b in range(BLOCKS):
+            if b < BLOCKS - 2:
+                p_now, value_now = pooled(b + 1)
+            elif b == BLOCKS - 2:
+                p_now, value_now = p_end, value_end
+            else:
+                p_now, value_now = p_after, None
+            pair_now = p + p_now
+            new = keep_own * value + (pair + pair_now)
+            st[(b + 1) * SUB : (b + 2) * SUB, :] = new
             e = jnp.exp2(new)
-            return acc[0] + e, acc[1] + e * e
-
-        def advance(ref, b, s, carry):
-            p, up, down, before, value, acc = carry
-            p_now, up_now, down_now, value_now = pooled(ref, s)
-            acc = finish(b * STRIP_UNROLL + s - 1, p, up, before, down, down_now, value, acc)
-            return p_now, up_now, down_now, up, value_now, acc
-
-        def block_ref(b):
-            at = pl.ds(pl.multiple_of(b * (STRIP_UNROLL * SUB), SUB), (STRIP_UNROLL + 2) * SUB)
-            return st.at[at, :]
-
-        def loop(b, carry):
-            ref = block_ref(b)
-            for k in range(STRIP_UNROLL):
-                carry = advance(ref, b, k, carry)
-            return carry
-
-        ref = block_ref(0)
-        p, up, down, value = pooled(ref, 0)
-        carry = p, up, down, p, value, (none, none)
-        for k in range(1, STRIP_UNROLL):
-            carry = advance(ref, jnp.int32(0), k, carry)
-        p, up, down, before, value, acc = lax.fori_loop(1, BLOCKS // STRIP_UNROLL, loop, carry)
-        return finish(jnp.int32(BLOCKS - 1), p, up, before, down, p, value, acc)
+            s1, s2 = s1 + e, s2 + e * e
+            p, value, pair = p_now, value_now, pair_now
+        return s1, s2
 
     lax.fori_loop(0, ITERS, strip_step, (s1, s2))
 
@@ -475,8 +478,8 @@
 
     @pl.when(has_right)
     def _():
-        for copy in tile_copies:
-            copy.wait_send()
+        high_copy.wait_send()
+        low_copy.wait_send()
         strip_right.wait_send()
 
     @pl.when(has_left)
@@ -524,11 +527,14 @@
             pltpu.VMEM((channels, rows, tile), jnp.bfloat16),
             pltpu.VMEM((channels, rows, tile), jnp.bfloat16),
             pltpu.VMEM((rows, tile), jnp.int32),
-            pltpu.VMEM((channels, rows, tile), jnp.bfloat16),
+            pltpu.VMEM((channels, rows, LANES), jnp.bfloat16),
+            pltpu.VMEM((channels // 2, rows, LANES), jnp.bfloat16),
+            pltpu.VMEM((channels // 2, rows, LANES), jnp.bfloat16),
             pltpu.VMEM((2, channels * SUB, LANES), f32),
             pltpu.VMEM((4, 4, channels * SUB, LANES), f32),
             pltpu.VMEM((SUB, 2 * tile, LANES), f32),
-            pltpu.VMEM((SUB, tile - 8, tile), f32),
+            pltpu.VMEM((SUB, 8 * channels, tile), jnp.bfloat16),
+            pltpu.VMEM((SUB, tile - 8 + D, tile), f32),
             pltpu.VMEM((2, SUB * PITCH, LANES), f32),
             pltpu.VMEM((strips, SUB, LANES), f32),
             pltpu.VMEM((strips // 4, SUB, LANES), f32),

time: 17.7 us -> 17 us (0.960)
  Pallas kernels: 16.3 us -> 15.5 us
    pallas_call x1, Pallas kernels: 14 us -> 13.2 us  [on_device(): pl.pallas_call(functools.partial(kernel, n), out_shape=(jax.ShapeDtypeStr...]
where the time goes in v3:
time: 17 us; the launch traced here: 16.8 us
  Pallas kernels  15.5 us (91%)
  between operations  1.28 us (8%)
    pallas_call x1, Pallas kernels, on_device(): pl.pallas_call(functools.partial(kernel, n), out_shape=(jax.ShapeDtypeStr...  13.2 us
    pallas_call x1, Pallas kernels, on_device(): pl.pallas_call(last_kernel, out_shape=(jax.ShapeDtypeStruct((rows, tile),...  2.33 us

profile of v3, /device:TPU:16, one launch (start us, length us, event | category | flops | bytes accessed | tf_op | source)
XLA Modules:
  0.0 16.8 jit_solution(16628433022525221592)
XLA Ops:
  1.3 13.2 %shard_map.59 = (f32[2,1552,128]{2,1,0:T(8,128)S(1)}, f32[400,128]{1,0:T(8,128)S(1)}, f32[9,8,256]{2,1,0:T(8,128)S(1)}, f32[4,8,128]{2,1,0:T(8,128)S(1)}, f32[8,256]{1,0:T(8,128)S(1)}) custom-call(bf16[32,8,256]{2,1,0:T(8,128)(2,1)} %left_hbm.1, bf16[32,8,256]{2,1,0:T(8,128)(2,1)} %right_hbm.1, s32[8,256]{1,0:T(8,128)} %mask_hbm.1, s32[1]{0:T(128)S(6)} %copy.6.offs_ref), custom_call_target="tpu_custom_call" | custom-call | tf_op jit(solution)/shard_map/pallas_call | solution.py:515
  14.5 2.3 %shard_map.60 = (f32[8,256]{1,0:T(8,128)}, bf16[192,8,256]{2,1,0:T(8,128)(2,1)}) custom-call(f32[8,256]{1,0:T(8,128)S(1)} %get-tuple-element.7.usable_ref, f32[2,1552,128]{2,1,0:T(8,128)S(1)} %get-tuple-element.8.v, f32[400,128]{1,0:T(8,128)S(1)} %get-tuple-element.9.st, f32[9,8,256]{2,1,0:T(8,128)S(1)} %get-tuple-element.10.w_ref, ...), custom_call_target="tpu_custom_call" | custom-call | tf_op jit(solution)/shard_map/pallas_call | solution.py:555

commit v4 on v3

--- a/solution.py
+++ b/solution.py
@@ -20,7 +20,6 @@
 PER = LANES // GROUP
 BLOCKS = D // PER
 LOG2E = math.log2(math.e)
-FIRST_UNROLL = 48
 UNROLL = 192
 PUT = 16
 CHANNEL_UNROLL = 32
@@ -65,9 +64,13 @@
     return out
 
 
+def gate(s1, s2):
+    purity = D * s2 / (s1 * s1)
+    return purity / (1.0 + purity)
+
+
 def coefficients(weights, usable, s1, s2):
-    purity = D * s2 / (s1 * s1)
-    gating = purity / (1.0 + purity)
+    gating = gate(s1, s2)
     part = 0.25 * usable * (1.0 - gating)
     return {k: lroll(weights[k] * part, k[0]) for k in STEPS}, usable * gating
 
@@ -172,7 +175,7 @@
 def kernel(
     n, left_hbm, right_hbm, mask_hbm, offs_ref, v, st, w_ref, sums_ref, usable_ref,
     left_ref, right_ref, mask_ref,
-    high, low_out, low_in, lf, rs, t4, rhs_ref, part, u, own, sent, from_left, from_right, load_sem, send_sem, recv_sem,
+    high, low_out, low_in, lf, rs, t4, rhs_ref, part, u, own, edge_sent, edge_left, edge_right, sent, from_left, from_right, load_sem, send_sem, recv_sem,
 ):
     channels = left_ref.shape[0]
     tile = left_ref.shape[2]
@@ -193,7 +196,7 @@
     loads = [
         pltpu.make_async_copy(src, dst, load_sem.at[i])
         for i, (src, dst) in enumerate((
-            (left_hbm, left_ref), (right_hbm, right_ref), (mask_hbm, mask_ref)
+            (right_hbm, right_ref), (left_hbm, left_ref), (mask_hbm, mask_ref)
         ))
     ]
     for load in loads:
@@ -204,10 +207,12 @@
         high[...] = jnp.zeros(high.shape, high.dtype)
         low_in[...] = jnp.zeros(low_in.shape, low_in.dtype)
         from_left[...] = jnp.zeros(from_left.shape, jnp.float32)
+        edge_left[...] = jnp.zeros(edge_left.shape, jnp.float32)
 
     @pl.when(jnp.logical_not(has_right))
     def _():
         from_right[...] = jnp.zeros(from_right.shape, jnp.float32)
+        edge_right[...] = jnp.zeros(edge_right.shape, jnp.float32)
 
     def remote(src, dst, slot, to):
         return pltpu.make_async_remote_copy(
@@ -215,25 +220,28 @@
             device_id={"col": to}, device_id_type=MESH,
         )
 
-    high_copy = remote(right_hbm.at[:, :, pl.ds(LANES, LANES)], high, 2, me + 1)
+    high_copy = remote(right_ref.at[:, :, pl.ds(LANES, LANES)], high, 2, me + 1)
     low_copy = remote(low_out, low_in, 3, me + 1)
-    strip_right = remote(sent, from_left, 0, me + 1)
-    strip_left = remote(sent, from_right, 1, me - 1)
+    strip_right = remote(sent.at[1], from_left, 0, me + 1)
+    strip_left = remote(sent.at[0], from_right, 1, me - 1)
+    edge_right_copy = remote(edge_sent.at[1], edge_left, 4, me + 1)
+    edge_left_copy = remote(edge_sent.at[0], edge_right, 5, me - 1)
 
     pl.semaphore_wait(barrier, has_left.astype(jnp.int32) + has_right.astype(jnp.int32))
 
+    loads[0].wait()
+
     @pl.when(has_right)
     def _():
         high_copy.start()
 
-    loads[1].wait()
     half = channels // 2
     for c in range(half):
         lead = right_ref[c, :, :LANES].astype(jnp.float32)
         trail = right_ref[c + half, :, :LANES].astype(jnp.float32)
         low_out[c] = jnp.where(lane < LANES // 2, lroll(lead, LANES // 2), trail).astype(low_out.dtype)
 
-    for load in (loads[0], loads[2]):
+    for load in loads[1:]:
         load.wait()
 
     usable = mask_ref[...].astype(jnp.float32)
@@ -277,6 +285,27 @@
     own[mask_at] = pack([(usable[:, :LANES], usable[:, LANES:])] * PER)
     for q in range(mask_at + 1, own.shape[0]):
         own[q] = jnp.zeros((SUB, LANES), jnp.float32)
+
+    place4 = (lane % GROUP) // 4
+
+    def gather(first, target):
+        for m in range(target.shape[1]):
+            for side, at in ((0, 1), (1, 6)):
+                out = own[first + 8 * m + at]
+                for i in range(8):
+                    if i != at:
+                        out = jnp.where(place4 == i, lroll(own[first + 8 * m + i], 4 * (i - at)), out)
+                target[side, m] = out
+
+    gather(BLOCKS, edge_sent)
+
+    @pl.when(has_right)
+    def _():
+        edge_right_copy.start()
+
+    @pl.when(has_left)
+    def _():
+        edge_left_copy.start()
 
     def own_part(t):
         return lambda c: right_ref[c, :, t * LANES : (t + 1) * LANES].astype(jnp.float32)
@@ -356,7 +385,8 @@
 
     scale = LOG2E / math.sqrt(channels)
     reach = offs_ref[0] * tile
-    half = [usable[:, :LANES], usable[:, LANES:]]
+    limit = [lane + (reach + t * LANES) for t in range(2)]
+    factor = [usable[:, t * LANES : (t + 1) * LANES] * scale for t in range(2)]
     none = jnp.zeros((SUB, LANES), jnp.float32)
     for t in range(2):
         v[t, :SUB, :] = none
@@ -364,35 +394,25 @@
     st[:SUB, :] = none
     st[(BLOCKS + 1) * SUB :, :] = none
 
-    def first(i, sums):
-        sums = list(sums)
-        for h in range(FIRST_UNROLL):
-            b = i * FIRST_UNROLL + h
-            planes = []
-            for s in range(PER):
-                j = s * BLOCKS + b
-                pair = []
-                for t in range(2):
-                    corr = u[t, pl.ds(j, SUB, stride=PITCH), :] * scale
-                    allowed = lane >= (D - 1 - j) - reach - t * LANES
-                    value = jnp.where(allowed, corr, FLOOR_COST * LOG2E) * half[t]
-                    v[t, pl.ds(pl.multiple_of((j + 1) * SUB, SUB), SUB), :] = value
-                    e = jnp.exp2(value)
-                    sums[2 * t] += e
-                    sums[2 * t + 1] += e * e
-                    pair.append(value)
-                planes.append(pair)
-            own[b] = pack(planes)
-        return tuple(sums)
-
-    sums = lax.fori_loop(0, BLOCKS // FIRST_UNROLL, first, (none,) * 4)
-
-    place4 = (lane % GROUP) // 4
-    for m in range(sent.shape[0]):
-        out = own[4 * m]
-        for s, (p, q) in ((1, (3, 0)), (2, (5, 2)), (3, (7, 4))):
-            out = jnp.where((place4 == p) | (place4 == q), lroll(own[4 * m + s], 8 * s), out)
-        sent[m] = out
+    sums = [none] * 4
+    for b in range(BLOCKS):
+        planes = []
+        for s in range(PER):
+            j = s * BLOCKS + b
+            pair = []
+            for t in range(2):
+                corr = u[t, pl.ds(j, SUB, stride=PITCH), :]
+                value = jnp.where(limit[t] >= D - 1 - j, corr, FLOOR_COST * LOG2E / scale) * factor[t]
+                v[t, (j + 1) * SUB : (j + 2) * SUB, :] = value
+                e = jnp.exp2(value)
+                sums[2 * t] += e
+                sums[2 * t + 1] += e * e
+                pair.append(value)
+            planes.append(pair)
+        own[b] = pack(planes)
+    sums = tuple(sums)
+
+    gather(0, sent)
 
     @pl.when(has_right)
     def _():
@@ -408,47 +428,45 @@
 
     @pl.when(has_left)
     def _():
+        edge_right_copy.wait_recv()
         strip_right.wait_recv()
 
     @pl.when(has_right)
     def _():
+        edge_left_copy.wait_recv()
         strip_left.wait_recv()
 
-    place = lane % GROUP
-
-    def joined(m, s):
-        out = jnp.where(place < 4, lroll(from_left[m], -24 - 8 * s), own[4 * m + s])
-        return jnp.where(place >= 28, lroll(from_right[m], 24 - 8 * s), out)
+    def joined(left, right, first, b):
+        m, i = divmod(b, 8)
+        out = jnp.where(place4 == 0, lroll(left[m], -4 * i), own[first + b])
+        return jnp.where(place4 == 7, lroll(right[m], 4 * (7 - i)), out)
 
     def over_groups(x):
-        x = x + lroll(x, GROUP)
-        return x + lroll(x, 2 * GROUP)
-
-    s1, s2 = none, none
-    for m in range(BLOCKS // 4):
-        for s in range(4):
-            value = joined(m, s)
-            st[(4 * m + s + 1) * SUB : (4 * m + s + 2) * SUB, :] = value
-            e = jnp.exp2(value)
-            s1, s2 = s1 + e, s2 + e * e
+        return (x + lroll(x, GROUP)) + (lroll(x, 2 * GROUP) + lroll(x, 3 * GROUP))
+
     strip_sums = (none,) * 5
     for q in range(channels // PER):
-        at = BLOCKS + q
         strip_sums = [
-            a + d for a, d in zip(strip_sums, distances(joined(at // 4, at % 4)))
+            a + d for a, d in zip(strip_sums, distances(joined(edge_left, edge_right, BLOCKS, q)))
         ]
     strip_weights = affinity([over_groups(x) for x in strip_sums], channels)
-    strip_usable = joined(mask_at // 4, mask_at % 4)
+    strip_weights = {k: lroll(strip_weights[k], k[0]) for k in STEPS}
+    strip_usable = joined(edge_left, edge_right, BLOCKS, channels // PER)
+    s1, s2 = none, none
+    for b in range(BLOCKS):
+        value = joined(from_left, from_right, 0, b)
+        st[(b + 1) * SUB : (b + 2) * SUB, :] = value
+        e = jnp.exp2(value)
+        s1, s2 = s1 + e, s2 + e * e
     lowest, highest = lane < GROUP, lane >= LANES - GROUP
 
     def strip_step(i, sums):
-        w, keep_own = coefficients(
-            strip_weights, strip_usable, over_groups(sums[0]), over_groups(sums[1])
-        )
+        gating = gate(over_groups(sums[0]), over_groups(sums[1]))
+        keep_own, part = strip_usable * gating, 0.25 * strip_usable * (1.0 - gating)
 
         def pooled(b):
             rows = three(st, b)
-            z = columns(w, *rows)
+            z = columns(strip_weights, *rows)
             return z[1] + (lroll(z[0], 1) + lroll(z[2], -1)), rows[1]
 
         p, value = pooled(0)
@@ -464,7 +482,7 @@
             else:
                 p_now, value_now = p_after, None
             pair_now = p + p_now
-            new = keep_own * value + (pair + pair_now)
+            new = keep_own * value + part * (pair + pair_now)
             st[(b + 1) * SUB : (b + 2) * SUB, :] = new
             e = jnp.exp2(new)
             s1, s2 = s1 + e, s2 + e * e
@@ -480,10 +498,12 @@
     def _():
         high_copy.wait_send()
         low_copy.wait_send()
+        edge_right_copy.wait_send()
         strip_right.wait_send()
 
     @pl.when(has_left)
     def _():
+        edge_left_copy.wait_send()
         strip_left.wait_send()
 
 
@@ -510,7 +530,8 @@
     channels, rows, tile = left_features.shape
     vmem = pl.BlockSpec(memory_space=pltpu.VMEM)
     hbm = pl.BlockSpec(memory_space=pltpu.HBM)
-    strips = -(-(BLOCKS + channels // PER + 1) // 4) * 4
+    edges = -(-(channels // PER + 1) // 8)
+    strips = BLOCKS + 8 * edges
     f32 = jnp.float32
     state = pl.pallas_call(
         functools.partial(kernel, n),
@@ -537,12 +558,15 @@
             pltpu.VMEM((SUB, tile - 8 + D, tile), f32),
             pltpu.VMEM((2, SUB * PITCH, LANES), f32),
             pltpu.VMEM((strips, SUB, LANES), f32),
-            pltpu.VMEM((strips // 4, SUB, LANES), f32),
-            pltpu.VMEM((strips // 4, SUB, LANES), f32),
-            pltpu.VMEM((strips // 4, SUB, LANES), f32),
+            pltpu.VMEM((2, edges, SUB, LANES), f32),
+            pltpu.VMEM((edges, SUB, LANES), f32),
+            pltpu.VMEM((edges, SUB, LANES), f32),
+            pltpu.VMEM((2, BLOCKS // 8, SUB, LANES), f32),
+            pltpu.VMEM((BLOCKS // 8, SUB, LANES), f32),
+            pltpu.VMEM((BLOCKS // 8, SUB, LANES), f32),
             pltpu.SemaphoreType.DMA((3,)),
-            pltpu.SemaphoreType.DMA((4,)),
-            pltpu.SemaphoreType.DMA((4,)),
+            pltpu.SemaphoreType.DMA((6,)),
+            pltpu.SemaphoreType.DMA((6,)),
         ],
         compiler_params=pltpu.CompilerParams(
             collective_id=0, has_side_effects=True, vmem_limit_bytes=VMEM_LIMIT

time: 17 us -> 15.9 us (0.935)
  Pallas kernels: 15.5 us -> 14.5 us
    pallas_call x1, Pallas kernels: 13.2 us -> 12.1 us  [on_device(): pl.pallas_call(functools.partial(kernel, n), out_shape=(jax.ShapeDtypeStr...]
where the time goes in v4:
time: 15.9 us; the launch traced here: 15.8 us
  Pallas kernels  14.5 us (91%)
  between operations  1.28 us (8%)
    pallas_call x1, Pallas kernels, on_device(): pl.pallas_call(functools.partial(kernel, n), out_shape=(jax.ShapeDtypeStr...  12.1 us
    pallas_call x1, Pallas kernels, on_device(): pl.pallas_call(last_kernel, out_shape=(jax.ShapeDtypeStruct((rows, tile),...  2.33 us

profile of v4, /device:TPU:16, one launch (start us, length us, event | category | flops | bytes accessed | tf_op | source)
XLA Modules:
  0.0 15.8 jit_solution(15634058391405221585)
XLA Ops:
  1.3 12.1 %shard_map.59 = (f32[2,1552,128]{2,1,0:T(8,128)S(1)}, f32[400,128]{1,0:T(8,128)S(1)}, f32[9,8,256]{2,1,0:T(8,128)S(1)}, f32[4,8,128]{2,1,0:T(8,128)S(1)}, f32[8,256]{1,0:T(8,128)S(1)}) custom-call(bf16[32,8,256]{2,1,0:T(8,128)(2,1)} %left_hbm.1, bf16[32,8,256]{2,1,0:T(8,128)(2,1)} %right_hbm.1, s32[8,256]{1,0:T(8,128)} %mask_hbm.1, s32[1]{0:T(128)S(6)} %copy.6.offs_ref), custom_call_target="tpu_custom_call" | custom-call | tf_op jit(solution)/shard_map/pallas_call | solution.py:536
  13.4 2.3 %shard_map.60 = (f32[8,256]{1,0:T(8,128)}, bf16[192,8,256]{2,1,0:T(8,128)(2,1)}) custom-call(f32[8,256]{1,0:T(8,128)S(1)} %get-tuple-element.7.usable_ref, f32[2,1552,128]{2,1,0:T(8,128)S(1)} %get-tuple-element.8.v, f32[400,128]{1,0:T(8,128)S(1)} %get-tuple-element.9.st, f32[9,8,256]{2,1,0:T(8,128)S(1)} %get-tuple-element.10.w_ref, ...), custom_call_target="tpu_custom_call" | custom-call | tf_op jit(solution)/shard_map/pallas_call | solution.py:579

commit v5 on v4

--- a/solution.py
+++ b/solution.py
@@ -22,7 +22,6 @@
 LOG2E = math.log2(math.e)
 UNROLL = 192
 PUT = 16
-CHANNEL_UNROLL = 32
 VMEM_LIMIT = 24 * 1024 * 1024
 
 
@@ -84,14 +83,13 @@
     return ref[at - 1 : at - 1 + SUB, :], ref[at : at + SUB, :], ref[at + 1 : at + 1 + SUB, :]
 
 
-def pack(planes):
+def pack(planes, side, out):
     lane = iota((SUB, LANES), 1)
     place = lane % GROUP
-    out = jnp.zeros((SUB, LANES), jnp.float32)
-    for s, (head, tail) in enumerate(planes):
-        mine = lane // GROUP == s
-        out = jnp.where(mine & (place >= 4) & (place < 16), lroll(head, GROUP * s + 4), out)
-        out = jnp.where(mine & (place >= 16) & (place < 28), lroll(tail, GROUP * s + 16 - 116), out)
+    low, shift = ((4, 4), (16, 16 - 116))[side]
+    here = (place >= low) & (place < low + 12)
+    for s, plane in enumerate(planes):
+        out = jnp.where((lane // GROUP == s) & here, lroll(plane, GROUP * s + shift), out)
     return out
 
 
@@ -175,7 +173,7 @@
 def kernel(
     n, left_hbm, right_hbm, mask_hbm, offs_ref, v, st, w_ref, sums_ref, usable_ref,
     left_ref, right_ref, mask_ref,
-    high, low_out, low_in, lf, rs, t4, rhs_ref, part, u, own, edge_sent, edge_left, edge_right, sent, from_left, from_right, load_sem, send_sem, recv_sem,
+    high_out, high, low_out, low_in, lf, rf, t4, rhs_ref, part, u, own, edge_w, edge_now, edge_sent, edge_left, edge_right, sent, from_left, from_right, load_sem, send_sem, recv_sem,
 ):
     channels = left_ref.shape[0]
     tile = left_ref.shape[2]
@@ -220,123 +218,128 @@
             device_id={"col": to}, device_id_type=MESH,
         )
 
-    high_copy = remote(right_ref.at[:, :, pl.ds(LANES, LANES)], high, 2, me + 1)
-    low_copy = remote(low_out, low_in, 3, me + 1)
+    halves = [pl.ds(i * SUB // 2, SUB // 2) for i in range(2)]
+    high_copies = [remote(high_out.at[h], high.at[h], 2 + i, me + 1) for i, h in enumerate(halves)]
+    low_copy = remote(low_out, low_in, 6, me + 1)
     strip_right = remote(sent.at[1], from_left, 0, me + 1)
     strip_left = remote(sent.at[0], from_right, 1, me - 1)
     edge_right_copy = remote(edge_sent.at[1], edge_left, 4, me + 1)
     edge_left_copy = remote(edge_sent.at[0], edge_right, 5, me - 1)
 
-    pl.semaphore_wait(barrier, has_left.astype(jnp.int32) + has_right.astype(jnp.int32))
-
-    loads[0].wait()
-
-    @pl.when(has_right)
-    def _():
-        high_copy.start()
-
-    half = channels // 2
-    for c in range(half):
-        lead = right_ref[c, :, :LANES].astype(jnp.float32)
-        trail = right_ref[c + half, :, :LANES].astype(jnp.float32)
-        low_out[c] = jnp.where(lane < LANES // 2, lroll(lead, LANES // 2), trail).astype(low_out.dtype)
-
-    for load in loads[1:]:
+    for load in loads:
         load.wait()
+
+    for c in range(channels):
+        for t in range(2):
+            rf[t, c * SUB : (c + 1) * SUB, :] = right_ref[c, :, t * LANES : (t + 1) * LANES].astype(jnp.float32)
+
+    def own_row(t, y):
+        return rf[t, pl.ds(y, channels, stride=SUB), :]
+
+    wide_lane = iota((channels, LANES), 1)
+    for y in range(SUB):
+        high_out[y] = own_row(1, y).astype(high_out.dtype)
+    for y in range(0, SUB, 2):
+        pair = jnp.where(wide_lane < LANES // 2, lroll(own_row(0, y), LANES // 2), own_row(0, y + 1))
+        low_out[y // 2] = pair.astype(low_out.dtype)
 
     usable = mask_ref[...].astype(jnp.float32)
     usable_ref[...] = usable
 
+    for c in range(channels):
+        for t in range(2):
+            lf[t, c * SUB : (c + 1) * SUB, :] = left_ref[c, :, t * LANES : (t + 1) * LANES].astype(jnp.float32)
+
+    none = jnp.zeros((SUB, LANES), jnp.float32)
+    for q in range(channels // PER):
+        out = none
+        for t in range(2):
+            rows = range(q * PER, (q + 1) * PER)
+            out = pack([lf[t, c * SUB : (c + 1) * SUB, :] for c in rows], t, out)
+        own[BLOCKS + q] = out
+    mask_at = BLOCKS + channels // PER
+    out = none
+    for t in range(2):
+        out = pack([usable[:, t * LANES : (t + 1) * LANES]] * PER, t, out)
+    own[mask_at] = out
+    for q in range(mask_at + 1, own.shape[0]):
+        own[q] = none
+
+    place4 = (lane % GROUP) // 4
+
+    def gather(first, target, m):
+        for side, at in ((0, 1), (1, 6)):
+            out = own[first + 8 * m + at]
+            for i in range(8):
+                if i != at:
+                    out = jnp.where(place4 == i, lroll(own[first + 8 * m + i], 4 * (i - at)), out)
+            target[side, m] = out
+
+    for m in range(edge_sent.shape[1]):
+        gather(BLOCKS, edge_sent, m)
+
+    pl.semaphore_wait(barrier, has_left.astype(jnp.int32) + has_right.astype(jnp.int32))
+
+    even = me % 2 == 0
+
+    @pl.when(has_left & even)
+    def _():
+        edge_left_copy.start()
+
+    @pl.when(has_right)
+    def _():
+        for copy in high_copies:
+            copy.start()
+        edge_right_copy.start()
+        low_copy.start()
+
+    @pl.when(has_left & jnp.logical_not(even))
+    def _():
+        edge_left_copy.start()
+
     zero = jnp.zeros((SUB, tile), jnp.float32)
 
-    def channel(c, sums):
-        plane = left_ref[c].astype(jnp.float32)
-        at = pl.ds(pl.multiple_of(c * SUB, SUB), SUB)
-        lf[0, at, :] = plane[:, :LANES]
-        lf[1, at, :] = plane[:, LANES:]
-        return tuple(s + d for s, d in zip(sums, distances(plane)))
-
-    per = CHANNEL_UNROLL
-
-    def unrolled(body):
-        def run(i, carry):
-            for k in range(per):
-                carry = body(i * per + k, carry)
-            return carry
-
-        return run
-
-    weights = affinity(lax.fori_loop(0, channels // per, unrolled(channel), (zero,) * 5), channels)
+    sums = (zero,) * 5
+    for c in range(channels):
+        sums = [s + d for s, d in zip(sums, distances(left_ref[c].astype(jnp.float32)))]
+    weights = affinity(sums, channels)
     for i, k in enumerate(STEPS):
         w_ref[i] = weights[k]
 
-    for q in range(channels // PER):
-        planes = [
-            (lf[0, (q * PER + s) * SUB : (q * PER + s + 1) * SUB, :],
-             lf[1, (q * PER + s) * SUB : (q * PER + s + 1) * SUB, :])
-            for s in range(PER)
-        ]
-        own[BLOCKS + q] = pack(planes)
-    @pl.when(has_right)
-    def _():
-        low_copy.start()
-
-    mask_at = BLOCKS + channels // PER
-    own[mask_at] = pack([(usable[:, :LANES], usable[:, LANES:])] * PER)
-    for q in range(mask_at + 1, own.shape[0]):
-        own[q] = jnp.zeros((SUB, LANES), jnp.float32)
-
-    place4 = (lane % GROUP) // 4
-
-    def gather(first, target):
-        for m in range(target.shape[1]):
-            for side, at in ((0, 1), (1, 6)):
-                out = own[first + 8 * m + at]
-                for i in range(8):
-                    if i != at:
-                        out = jnp.where(place4 == i, lroll(own[first + 8 * m + i], 4 * (i - at)), out)
-                target[side, m] = out
-
-    gather(BLOCKS, edge_sent)
-
-    @pl.when(has_right)
-    def _():
-        edge_right_copy.start()
-
-    @pl.when(has_left)
-    def _():
-        edge_left_copy.start()
-
-    def own_part(t):
-        return lambda c: right_ref[c, :, t * LANES : (t + 1) * LANES].astype(jnp.float32)
-
-    def high_part(c):
-        return high[c].astype(jnp.float32)
-
-    def low_part(c):
-        x = low_in[c % half].astype(jnp.float32)
-        return lroll(x, LANES // 2) if c < half else x
-
-    def shifts(t, part_of, next_of):
-        for c in range(channels):
-            now = part_of(c)
-            after = now if next_of is None else next_of(c)
-            for s in range(4):
-                value = lroll(jnp.where(lane < s, after, now), -s) if s else now
-                rs[s, t, c * SUB : (c + 1) * SUB, :] = value
+    def joined(left, right, first, b):
+        m, i = divmod(b, 8)
+        out = jnp.where(place4 == 0, lroll(left[m], -4 * i), own[first + b])
+        return jnp.where(place4 == 7, lroll(right[m], 4 * (7 - i)), out)
+
+    def over_groups(x):
+        return (x + lroll(x, GROUP)) + (lroll(x, 2 * GROUP) + lroll(x, 3 * GROUP))
+
+    def edge_weights(left, right):
+        sums = (none,) * 5
+        for q in range(channels // PER):
+            plane = joined(left, right, BLOCKS, q)
+            sums = [a + d for a, d in zip(sums, distances(plane))]
+        edge = affinity([over_groups(x) for x in sums], channels)
+        for i, k in enumerate(STEPS):
+            edge_w[i] = lroll(edge[k], k[0])
+        edge_w[len(STEPS)] = joined(left, right, BLOCKS, channels // PER)
+
+    def high_row(y):
+        return high[y].astype(jnp.float32)
+
+    def low_row(y):
+        x = low_in[y // 2].astype(jnp.float32)
+        return x if y % 2 else lroll(x, LANES // 2)
+
+    def turn(t, y, now, after):
+        block = [now] + [lroll(jnp.where(wide_lane < s, after, now), -s) for s in range(1, 4)]
+        t4[y, t * LANES : (t + 1) * LANES, :] = jnp.concatenate(block, axis=0).T
 
     depth = 8 * channels
     keep = (iota((depth, tile), 0) // channels == iota((depth, tile), 1) % 8).astype(jnp.bfloat16)
     rows_out = tile - 8 + D
     begin = tile - D + 1
     first_cut, second_cut = LANES // 2, D
-
-    def transposes(t):
-        for y in range(SUB):
-            block = jnp.concatenate(
-                [rs[s, t, pl.ds(y, channels, stride=SUB), :] for s in range(4)], axis=0
-            )
-            t4[y, t * LANES : (t + 1) * LANES, :] = block.T
 
     def scores_of(y, low, high, width):
         lhs = jnp.concatenate(
@@ -352,10 +355,9 @@
             x = jnp.where(on, x[bit:], x[:size])
         u[t, y * PITCH : y * PITCH + D, :] = x
 
-    shifts(2, own_part(0), own_part(1))
-    shifts(3, own_part(1), None)
-    transposes(2)
-    transposes(3)
+    for y in range(SUB):
+        turn(2, y, own_row(0, y), own_row(1, y))
+        turn(3, y, own_row(1, y), own_row(1, y))
     for y in range(SUB):
         l_row = jnp.concatenate(
             [lf[t, pl.ds(y, channels, stride=SUB), :] for t in range(2)], axis=1
@@ -363,56 +365,83 @@
         rhs_ref[y] = jnp.concatenate([l_row] * 8, axis=0) * keep
         part[y, second_cut:, :] = scores_of(y, second_cut, rows_out, tile)
 
+    for i, copy in enumerate(high_copies):
+        @pl.when(has_left)
+        def _():
+            copy.wait_recv()
+
+        rows = range(i * SUB // 2, (i + 1) * SUB // 2)
+        for y in rows:
+            turn(1, y, high_row(y), own_row(0, y))
+        for y in rows:
+            part[y, first_cut:second_cut, :] = scores_of(y, first_cut, second_cut, tile)
+            straighten(y, 1, part[y, LANES:, LANES:])
+
     @pl.when(has_left)
     def _():
-        high_copy.wait_recv()
-
-    shifts(1, high_part, own_part(0))
-    transposes(1)
-    for y in range(SUB):
-        part[y, first_cut:second_cut, :] = scores_of(y, first_cut, second_cut, tile)
-        straighten(y, 1, part[y, LANES:, LANES:])
-
-    @pl.when(has_left)
-    def _():
         low_copy.wait_recv()
 
-    shifts(0, low_part, high_part)
-    transposes(0)
-    for y in range(SUB):
-        x = scores_of(y, 0, first_cut, LANES)
-        straighten(y, 0, jnp.concatenate([x, part[y, first_cut : D + LANES - 8, :LANES]], axis=0))
+    def edges_arrived():
+        @pl.when(has_left)
+        def _():
+            edge_right_copy.wait_recv()
+
+        @pl.when(has_right)
+        def _():
+            edge_left_copy.wait_recv()
 
     scale = LOG2E / math.sqrt(channels)
     reach = offs_ref[0] * tile
-    limit = [lane + (reach + t * LANES) for t in range(2)]
-    factor = [usable[:, t * LANES : (t + 1) * LANES] * scale for t in range(2)]
-    none = jnp.zeros((SUB, LANES), jnp.float32)
     for t in range(2):
         v[t, :SUB, :] = none
         v[t, (D + 1) * SUB :, :] = none
     st[:SUB, :] = none
     st[(BLOCKS + 1) * SUB :, :] = none
 
-    sums = [none] * 4
-    for b in range(BLOCKS):
-        planes = []
-        for s in range(PER):
-            j = s * BLOCKS + b
-            pair = []
+    @pl.when(even)
+    def _():
+        edges_arrived()
+        edge_now[0] = edge_left[...]
+        edge_now[1] = edge_right[...]
+
+    @pl.when(jnp.logical_not(even))
+    def _():
+        edge_now[...] = jnp.zeros(edge_now.shape, jnp.float32)
+
+    for y in range(SUB):
+        turn(0, y, low_row(y), high_row(y))
+    edge_weights(edge_now.at[0], edge_now.at[1])
+    for y in range(SUB):
+        x = scores_of(y, 0, first_cut, LANES)
+        straighten(y, 0, jnp.concatenate([x, part[y, first_cut : D + LANES - 8, :LANES]], axis=0))
+
+    @pl.when(me >= 0)
+    def _():
+        limit = [lane + (reach + t * LANES) for t in range(2)]
+        factor = [usable[:, t * LANES : (t + 1) * LANES] * scale for t in range(2)]
+        sums = [none] * 4
+        for b in range(BLOCKS):
+            planes = []
+            for s in range(PER):
+                j = s * BLOCKS + b
+                pair = []
+                for t in range(2):
+                    corr = u[t, pl.ds(j, SUB, stride=PITCH), :]
+                    value = jnp.where(limit[t] >= D - 1 - j, corr, FLOOR_COST * LOG2E / scale) * factor[t]
+                    v[t, (j + 1) * SUB : (j + 2) * SUB, :] = value
+                    e = jnp.exp2(value)
+                    sums[2 * t] += e
+                    sums[2 * t + 1] += e * e
+                    pair.append(value)
+                planes.append(pair)
+            out = none
             for t in range(2):
-                corr = u[t, pl.ds(j, SUB, stride=PITCH), :]
-                value = jnp.where(limit[t] >= D - 1 - j, corr, FLOOR_COST * LOG2E / scale) * factor[t]
-                v[t, (j + 1) * SUB : (j + 2) * SUB, :] = value
-                e = jnp.exp2(value)
-                sums[2 * t] += e
-                sums[2 * t + 1] += e * e
-                pair.append(value)
-            planes.append(pair)
-        own[b] = pack(planes)
-    sums = tuple(sums)
-
-    gather(0, sent)
+                out = pack([pair[t] for pair in planes], t, out)
+            own[b] = out
+        for t in range(4):
+            sums_ref[t] = sums[t]
+        for m in range(sent.shape[1]):
+            gather(0, sent, m)
 
     @pl.when(has_right)
     def _():
@@ -423,35 +452,26 @@
         strip_left.start()
 
     sums = lax.fori_loop(
-        0, ITERS - 1, lambda i, s: step(v, st, w_ref, usable, None, s), sums
+        0, ITERS - 1, lambda i, s: step(v, st, w_ref, usable, None, s),
+        tuple(sums_ref[t] for t in range(4)),
     )
 
+    @pl.when(jnp.logical_not(even))
+    def _():
+        edges_arrived()
+        edge_weights(edge_left, edge_right)
+
     @pl.when(has_left)
     def _():
-        edge_right_copy.wait_recv()
         strip_right.wait_recv()
 
     @pl.when(has_right)
     def _():
-        edge_left_copy.wait_recv()
         strip_left.wait_recv()
 
-    def joined(left, right, first, b):
-        m, i = divmod(b, 8)
-        out = jnp.where(place4 == 0, lroll(left[m], -4 * i), own[first + b])
-        return jnp.where(place4 == 7, lroll(right[m], 4 * (7 - i)), out)
-
-    def over_groups(x):
-        return (x + lroll(x, GROUP)) + (lroll(x, 2 * GROUP) + lroll(x, 3 * GROUP))
-
-    strip_sums = (none,) * 5
-    for q in range(channels // PER):
-        strip_sums = [
-            a + d for a, d in zip(strip_sums, distances(joined(edge_left, edge_right, BLOCKS, q)))
-        ]
-    strip_weights = affinity([over_groups(x) for x in strip_sums], channels)
-    strip_weights = {k: lroll(strip_weights[k], k[0]) for k in STEPS}
-    strip_usable = joined(edge_left, edge_right, BLOCKS, channels // PER)
+    strip_weights = {k: edge_w[i] for i, k in enumerate(STEPS)}
+    strip_usable = edge_w[len(STEPS)]
+
     s1, s2 = none, none
     for b in range(BLOCKS):
         value = joined(from_left, from_right, 0, b)
@@ -496,7 +516,8 @@
 
     @pl.when(has_right)
     def _():
-        high_copy.wait_send()
+        for copy in high_copies:
+            copy.wait_send()
         low_copy.wait_send()
         edge_right_copy.wait_send()
         strip_right.wait_send()
@@ -548,16 +569,19 @@
             pltpu.VMEM((channels, rows, tile), jnp.bfloat16),
             pltpu.VMEM((channels, rows, tile), jnp.bfloat16),
             pltpu.VMEM((rows, tile), jnp.int32),
-            pltpu.VMEM((channels, rows, LANES), jnp.bfloat16),
-            pltpu.VMEM((channels // 2, rows, LANES), jnp.bfloat16),
-            pltpu.VMEM((channels // 2, rows, LANES), jnp.bfloat16),
+            pltpu.VMEM((rows, channels, LANES), jnp.bfloat16),
+            pltpu.VMEM((rows, channels, LANES), jnp.bfloat16),
+            pltpu.VMEM((rows // 2, channels, LANES), jnp.bfloat16),
+            pltpu.VMEM((rows // 2, channels, LANES), jnp.bfloat16),
             pltpu.VMEM((2, channels * SUB, LANES), f32),
-            pltpu.VMEM((4, 4, channels * SUB, LANES), f32),
+            pltpu.VMEM((2, channels * SUB, LANES), f32),
             pltpu.VMEM((SUB, 2 * tile, LANES), f32),
             pltpu.VMEM((SUB, 8 * channels, tile), jnp.bfloat16),
             pltpu.VMEM((SUB, tile - 8 + D, tile), f32),
             pltpu.VMEM((2, SUB * PITCH, LANES), f32),
             pltpu.VMEM((strips, SUB, LANES), f32),
+            pltpu.VMEM((len(STEPS) + 1, SUB, LANES), f32),
+            pltpu.VMEM((2, edges, SUB, LANES), f32),
             pltpu.VMEM((2, edges, SUB, LANES), f32),
             pltpu.VMEM((edges, SUB, LANES), f32),
             pltpu.VMEM((edges, SUB, LANES), f32),
@@ -565,8 +589,8 @@
             pltpu.VMEM((BLOCKS // 8, SUB, LANES), f32),
             pltpu.VMEM((BLOCKS // 8, SUB, LANES), f32),
             pltpu.SemaphoreType.DMA((3,)),
-            pltpu.SemaphoreType.DMA((6,)),
-            pltpu.SemaphoreType.DMA((6,)),
+            pltpu.SemaphoreType.DMA((7,)),
+            pltpu.SemaphoreType.DMA((7,)),
         ],
         compiler_params=pltpu.CompilerParams(
             collective_id=0, has_side_effects=True, vmem_limit_bytes=VMEM_LIMIT

time: 15.9 us -> 15.7 us (0.987)
  Pallas kernels: 14.5 us -> 14.3 us
    pallas_call x1, Pallas kernels: 12.1 us -> 12 us  [on_device(): pl.pallas_call(functools.partial(kernel, n), out_shape=(jax.ShapeDtypeStr...]
where the time goes in v5:
time: 15.7 us; the launch traced here: 15.6 us
  Pallas kernels  14.3 us (91%)
  between operations  1.28 us (8%)
    pallas_call x1, Pallas kernels, on_device(): pl.pallas_call(functools.partial(kernel, n), out_shape=(jax.ShapeDtypeStr...  12 us
    pallas_call x1, Pallas kernels, on_device(): pl.pallas_call(last_kernel, out_shape=(jax.ShapeDtypeStruct((rows, tile),...  2.33 us

profile of v5, /device:TPU:16, one launch (start us, length us, event | category | flops | bytes accessed | tf_op | source)
XLA Modules:
  0.0 15.6 jit_solution(8122802620739490308)
XLA Ops:
  1.3 12.0 %shard_map.59 = (f32[2,1552,128]{2,1,0:T(8,128)S(1)}, f32[400,128]{1,0:T(8,128)S(1)}, f32[9,8,256]{2,1,0:T(8,128)S(1)}, f32[4,8,128]{2,1,0:T(8,128)S(1)}, f32[8,256]{1,0:T(8,128)S(1)}) custom-call(bf16[32,8,256]{2,1,0:T(8,128)(2,1)} %left_hbm.1, bf16[32,8,256]{2,1,0:T(8,128)(2,1)} %right_hbm.1, s32[8,256]{1,0:T(8,128)} %mask_hbm.1, s32[1]{0:T(128)S(6)} %copy.6.offs_ref), custom_call_target="tpu_custom_call" | custom-call | tf_op jit(solution)/shard_map/pallas_call | solution.py:557
  13.3 2.3 %shard_map.60 = (f32[8,256]{1,0:T(8,128)}, bf16[192,8,256]{2,1,0:T(8,128)(2,1)}) custom-call(f32[8,256]{1,0:T(8,128)S(1)} %get-tuple-element.7.usable_ref, f32[2,1552,128]{2,1,0:T(8,128)S(1)} %get-tuple-element.8.v, f32[400,128]{1,0:T(8,128)S(1)} %get-tuple-element.9.st, f32[9,8,256]{2,1,0:T(8,128)S(1)} %get-tuple-element.10.w_ref, ...), custom_call_target="tpu_custom_call" | custom-call | tf_op jit(solution)/shard_map/pallas_call | solution.py:603

commit v6 on v5

--- a/solution.py
+++ b/solution.py
@@ -22,6 +22,7 @@
 LOG2E = math.log2(math.e)
 UNROLL = 192
 PUT = 16
+PIECES = 1
 VMEM_LIMIT = 24 * 1024 * 1024
 
 
@@ -218,8 +219,8 @@
             device_id={"col": to}, device_id_type=MESH,
         )
 
-    halves = [pl.ds(i * SUB // 2, SUB // 2) for i in range(2)]
-    high_copies = [remote(high_out.at[h], high.at[h], 2 + i, me + 1) for i, h in enumerate(halves)]
+    pieces = [pl.ds(i * SUB // PIECES, SUB // PIECES) for i in range(PIECES)]
+    high_copies = [remote(high_out.at[h], high.at[h], 2 + i, me + 1) for i, h in enumerate(pieces)]
     low_copy = remote(low_out, low_in, 6, me + 1)
     strip_right = remote(sent.at[1], from_left, 0, me + 1)
     strip_left = remote(sent.at[0], from_right, 1, me - 1)
@@ -370,7 +371,7 @@
         def _():
             copy.wait_recv()
 
-        rows = range(i * SUB // 2, (i + 1) * SUB // 2)
+        rows = range(i * SUB // PIECES, (i + 1) * SUB // PIECES)
         for y in rows:
             turn(1, y, high_row(y), own_row(0, y))
         for y in rows:

time: 15.7 us -> 15.8 us (level)
  no operation moved by 1% of the time
where the time goes in v6:
time: 15.8 us; the launch traced here: 15.6 us
  Pallas kernels  14.3 us (91%)
  between operations  1.28 us (8%)
    pallas_call x1, Pallas kernels, on_device(): pl.pallas_call(functools.partial(kernel, n), out_shape=(jax.ShapeDtypeStr...  12 us
    pallas_call x1, Pallas kernels, on_device(): pl.pallas_call(last_kernel, out_shape=(jax.ShapeDtypeStruct((rows, tile),...  2.33 us

profile of v6, /device:TPU:16, one launch (start us, length us, event | category | flops | bytes accessed | tf_op | source)
XLA Modules:
  0.0 15.6 jit_solution(16470251790138719060)
XLA Ops:
  1.3 12.0 %shard_map.59 = (f32[2,1552,128]{2,1,0:T(8,128)S(1)}, f32[400,128]{1,0:T(8,128)S(1)}, f32[9,8,256]{2,1,0:T(8,128)S(1)}, f32[4,8,128]{2,1,0:T(8,128)S(1)}, f32[8,256]{1,0:T(8,128)S(1)}) custom-call(bf16[32,8,256]{2,1,0:T(8,128)(2,1)} %left_hbm.1, bf16[32,8,256]{2,1,0:T(8,128)(2,1)} %right_hbm.1, s32[8,256]{1,0:T(8,128)} %mask_hbm.1, s32[1]{0:T(128)S(6)} %copy.6.offs_ref), custom_call_target="tpu_custom_call" | custom-call | tf_op jit(solution)/shard_map/pallas_call | solution.py:558
  13.3 2.3 %shard_map.60 = (f32[8,256]{1,0:T(8,128)}, bf16[192,8,256]{2,1,0:T(8,128)(2,1)}) custom-call(f32[8,256]{1,0:T(8,128)S(1)} %get-tuple-element.7.usable_ref, f32[2,1552,128]{2,1,0:T(8,128)S(1)} %get-tuple-element.8.v, f32[400,128]{1,0:T(8,128)S(1)} %get-tuple-element.9.st, f32[9,8,256]{2,1,0:T(8,128)S(1)} %get-tuple-element.10.w_ref, ...), custom_call_target="tpu_custom_call" | custom-call | tf_op jit(solution)/shard_map/pallas_call | solution.py:604
